TPU v7x, 512 devices: a whole 4x4x16 slice. The times are simulated.
512 devices in a mesh: patch: 128 (over z, y, core), visit: 4 (over x).
Axes of the slice: x: 4, y: 4, z: 16, core: 2. Of those that a mesh axis runs over, the one named last changes fastest.
Arguments:
- science: float32 [65536, 2, 128], P(('patch', 'visit')), may hold values from -40 to 40
- inverse_sigma: float32 [65536, 2, 128], P(('patch', 'visit')), may hold values from 0.24 to 3.6
- template: float32 [128, 256, 1024], P('patch', 'visit'), may hold values from -6 to 6
- destination: int32 [65536], P(('patch', 'visit')), may hold values from 0 to 127, as said below
- offsets: int32 [65536, 2], P(('patch', 'visit')), may hold values from 0 to 876, as said below
- visit_local: int32 [65536], P(('patch', 'visit')), may hold values from 0 to 15, as said below
Outputs:
- difference: float32 [65536, 2, 128], P(('patch', 'visit'))
- coefficients: float32 [64, 28], P('visit')
Inputs may be any that keep to these rules, and one draw needn't show every extreme that they name: `destination`: in each aligned block of 128 rows no patch is named more than 2 times, and in every draw some patch is named exactly 2 times in every block. `offsets`: column 0 is at most 234, column 1 at most 876. `visit_local`: each aligned block of 128 rows holds every value exactly 128 // 16 times.
All inputs are finite; a program needn't handle non-finite values.
Results may differ from a plain program's by a relative error of at most 0.0098.
Values may be sent and summed in bfloat16 or wider, within the bound.
No kernel may reach another device: no remote copies, remote signals or barrier semaphores. Data moves between devices by JAX's collectives and lax.ppermute only.
A program may use at most 64 MiB of HBM per device.

v0:
```python
import math

import jax
import jax.numpy as jnp
import numpy as np
from jax import lax
from jax.sharding import PartitionSpec as P

KR = 10
NF = 11
NB = 28
VIS_DEV = 16


gauss_widths = (1.0, 2.0, 4.0)
poly_degrees = (4, 2, 2)


def as_sent(array):
    return jax.tree.map(lambda a: a.astype(jnp.bfloat16) if a.dtype == jnp.float32 else a, array)


def filter_table(radius):
    tap_points = np.arange(-radius, radius + 1) * 1.0
    raw_columns = []
    for width_value, degree in zip(gauss_widths, poly_degrees):
        bell_curve = np.exp(-tap_points * tap_points / (2.0 * width_value * width_value))
        for power_index in range(degree + 1):
            raw_columns.append(bell_curve * (tap_points / radius) ** power_index)
    orthonormal = []
    for column in raw_columns:
        vector = column.copy()
        for repeat_index in range(2):
            for earlier in orthonormal:
                vector = vector - np.dot(earlier, vector) * earlier
        orthonormal.append(vector / np.sqrt(np.dot(vector, vector)))
    return np.stack(orthonormal, axis=1).astype(np.float32)


def pair_layout():
    column_ids = []
    row_ids = []
    filter_runs = []
    offset = 0
    for degree in poly_degrees:
        for first_index in range(degree + 1):
            filter_runs.append((offset + first_index, offset, offset + degree - first_index + 1))
            for second_index in range(degree + 1 - first_index):
                column_ids.append(offset + first_index)
                row_ids.append(offset + second_index)
        offset += degree + 1
    return (column_ids, row_ids, filter_runs)


def build_tables(row_count, column_count):
    values = filter_table(KR)
    filters = values.shape[1]
    taps_count = 2 * KR + 1
    row_band = np.zeros((filters, row_count, row_count + 2 * KR), np.float32)
    for out_row in range(row_count):
        row_band[:, out_row, out_row : out_row + taps_count] = values.T
    column_band = np.zeros((filters, column_count + 2 * KR, column_count), np.float32)
    for out_column in range(column_count):
        column_band[:, out_column : out_column + taps_count, out_column] = values.T
    row_matrix = jnp.asarray(row_band.reshape(filters * row_count, row_count + 2 * KR)).astype(
        jnp.bfloat16
    )
    column_matrix = jnp.asarray(column_band).astype(jnp.bfloat16)
    tap_values = lax.optimization_barrier(jnp.asarray(values).astype(jnp.bfloat16)).astype(
        jnp.float32
    )
    return (row_matrix, column_matrix, tap_values)


def slice_windows(whole, row_starts, column_starts, height, breadth):

    def one_window(row_at, column_at):
        return lax.dynamic_slice(whole, (row_at, column_at), (height, breadth))

    return jax.vmap(one_window)(row_starts, column_starts)


def filtered_block(windows, row_matrix):
    count_items = windows.shape[0]
    row_count = row_matrix.shape[0] // NF
    product = jnp.einsum("ry,nyx->nrx", row_matrix, windows, preferred_element_type=jnp.float32)
    return product.astype(jnp.bfloat16).reshape(count_items, NF, row_count, windows.shape[2])


def fit_block(
    windows, block_scaled, block_weights, block_visits, block_live, row_matrix, column_matrix
):
    count_items = windows.shape[0]
    filtered = filtered_block(windows, row_matrix)
    column_ids, row_ids, filter_runs = pair_layout()
    pieces_list = []
    for column_id, low_row, high_row in filter_runs:
        pieces_list.append(
            jnp.einsum(
                "nbix,xj->nbij",
                filtered[:, low_row:high_row],
                column_matrix[column_id],
                preferred_element_type=jnp.float32,
            )
        )
    images = jnp.concatenate(pieces_list, axis=1)
    weight_values = block_weights.astype(jnp.float32)
    design = (images * weight_values[:, None]).astype(jnp.bfloat16)
    design = jnp.concatenate([design, block_weights[:, None]], axis=1).reshape(count_items, NB, -1)
    gram_matrix = jnp.einsum("nkp,nlp->nkl", design, design, preferred_element_type=jnp.float32)
    right_vector = jnp.einsum(
        "nkp,np->nk",
        design,
        block_scaled.reshape(count_items, -1),
        preferred_element_type=jnp.float32,
    )
    member = (block_visits[:, None] == jnp.arange(VIS_DEV, dtype=jnp.int32)[None, :]) & (
        block_live[:, None] > 0
    )
    member = jnp.where(member, 1.0, 0.0).astype(jnp.float32)
    gram_visit = jnp.einsum("nv,nkl->vkl", member, gram_matrix, precision=lax.Precision.HIGHEST)
    right_visit = jnp.einsum("nv,nk->vk", member, right_vector, precision=lax.Precision.HIGHEST)
    return (gram_visit, right_visit)


def model_block(windows, block_visits, coefficients, mixing, row_matrix, tap_values):
    filtered = filtered_block(windows, row_matrix)
    column_count = windows.shape[2] - 2 * KR
    combined = jnp.einsum(
        "nab,nbix->naix",
        jnp.take(mixing, block_visits, axis=0),
        filtered.astype(jnp.float32),
        precision=lax.Precision.HIGHEST,
    )
    model = jnp.take(coefficients[:, NB - 1], block_visits)[:, None, None] + jnp.zeros(
        combined.shape[:1] + combined.shape[2:3] + (column_count,), jnp.float32
    )
    for shift_index in range(2 * KR + 1):
        weighted = (
            combined[..., shift_index : shift_index + column_count]
            * tap_values[shift_index][None, :, None, None]
        )
        model = model + jnp.sum(weighted, axis=1)
    return model.astype(jnp.bfloat16)


def in_blocks(function, arrays, block_size):
    total_rows = arrays[0].shape[0]
    shaped = tuple(
        (
            values.reshape((total_rows // block_size, block_size) + values.shape[1:])
            for values in arrays
        )
    )
    return lax.map(lambda pieces: function(*pieces), shaped)


def visit_sums(windows, scaled, weights, visits, live, row_matrix, column_matrix):
    block_size = math.gcd(windows.shape[0], 32)

    def visit_one_block(part_windows, part_scaled, part_weights, part_visits, part_live):
        return fit_block(
            part_windows,
            part_scaled,
            part_weights,
            part_visits,
            part_live,
            row_matrix,
            column_matrix,
        )

    block_gram_list, right_blocks = in_blocks(
        visit_one_block, (windows, scaled, weights, visits, live), block_size
    )
    return (jnp.sum(block_gram_list, axis=0), jnp.sum(right_blocks, axis=0))


def fit_coefficients(gram_total, right_total):
    gram_total, right_total = lax.psum((gram_total, right_total), "patch")
    factor = jnp.linalg.cholesky(gram_total)
    return jax.scipy.linalg.cho_solve((factor, True), right_total[..., None])[..., 0]


def model_all(windows, visits, coefficients, row_matrix, tap_values):
    column_ids, row_ids, filter_runs = pair_layout()
    column_index = jnp.asarray(column_ids, dtype=jnp.int32)
    row_index = jnp.asarray(row_ids, dtype=jnp.int32)
    mixing = (
        jnp.zeros((VIS_DEV, NF, NF), jnp.float32)
        .at[:, column_index, row_index]
        .set(coefficients[:, : NB - 1])
    )
    block_size = math.gcd(windows.shape[0], 32)

    def model_one_block(part_windows, part_visits):
        return model_block(part_windows, part_visits, coefficients, mixing, row_matrix, tap_values)

    model = in_blocks(model_one_block, (windows, visits), block_size)
    return model.reshape((windows.shape[0],) + model.shape[2:])


def per_device(science, inverse_sigma, template, destination, offsets, visit_local):
    patches = lax.axis_size("patch")
    tile_count, row_count, column_count = science.shape
    capacity = max(2, 2 * tile_count // patches)
    slot_count = patches * capacity
    height = row_count + 2 * KR
    breadth = column_count + 2 * KR
    row_matrix, column_matrix, tap_values = build_tables(row_count, column_count)
    gathered = lax.all_gather(template.astype(jnp.bfloat16), "visit", axis=1, tiled=True)
    whole_template = gathered[0]
    order_ids = jnp.arange(tile_count, dtype=jnp.int32)
    same_patch = destination[:, None] == destination[None, :]
    before = order_ids[None, :] < order_ids[:, None]
    tile_rank = jnp.sum(jnp.where(same_patch & before, 1, 0), axis=1).astype(jnp.int32)
    slot_of_tile = destination * capacity + tile_rank
    slot_ids = jnp.arange(slot_count, dtype=jnp.int32)
    holds = slot_of_tile[None, :] == slot_ids[:, None]
    filled = jnp.any(holds, axis=1)
    source_tile = jnp.sum(jnp.where(holds, order_ids[None, :], 0), axis=1)
    weights = inverse_sigma.astype(jnp.bfloat16)
    scaled_science = (science * inverse_sigma).astype(jnp.bfloat16)
    zero_tile = jnp.zeros((), jnp.bfloat16)
    packed_science = jnp.where(
        filled[:, None, None], jnp.take(scaled_science, source_tile, axis=0), zero_tile
    )
    packed_weights = jnp.where(
        filled[:, None, None], jnp.take(weights, source_tile, axis=0), zero_tile
    )
    details = jnp.stack(
        [
            jnp.where(filled, 1, 0).astype(jnp.int32),
            jnp.take(visit_local, source_tile),
            jnp.take(offsets[:, 0], source_tile),
            jnp.take(offsets[:, 1], source_tile),
        ],
        axis=1,
    )
    details = jnp.where(filled[:, None], details, 0)
    arrived_science, arrived_weights, arrived_details = (
        lax.all_to_all(
            packed_science.reshape(patches, capacity, row_count, column_count),
            "patch",
            split_axis=0,
            concat_axis=0,
            tiled=True,
        ),
        lax.all_to_all(
            packed_weights.reshape(patches, capacity, row_count, column_count),
            "patch",
            split_axis=0,
            concat_axis=0,
            tiled=True,
        ),
        lax.all_to_all(
            details.reshape(patches, capacity, 4), "patch", split_axis=0, concat_axis=0, tiled=True
        ),
    )
    arrived_science = arrived_science.reshape(slot_count, row_count, column_count)
    arrived_weights = arrived_weights.reshape(slot_count, row_count, column_count)
    arrived_details = arrived_details.reshape(slot_count, 4)
    windows = slice_windows(
        whole_template, arrived_details[:, 2], arrived_details[:, 3], height, breadth
    )
    gram_total, right_total = visit_sums(
        windows,
        arrived_science,
        arrived_weights,
        arrived_details[:, 1],
        arrived_details[:, 0],
        row_matrix,
        column_matrix,
    )
    coefficients = fit_coefficients(gram_total, right_total)
    model = model_all(windows, arrived_details[:, 1], coefficients, row_matrix, tap_values)
    returned = lax.all_to_all(
        as_sent(model.reshape(patches, capacity, row_count, column_count)),
        "patch",
        split_axis=0,
        concat_axis=0,
        tiled=True,
    )
    own_model = jnp.take(
        returned.reshape(slot_count, row_count, column_count), slot_of_tile, axis=0
    )
    difference = science - lax.optimization_barrier(own_model).astype(jnp.float32)
    return (difference, coefficients)


def solution(mesh):
    return jax.shard_map(
        per_device,
        mesh=mesh,
        in_specs=(
            P(("patch", "visit"), None, None),
            P(("patch", "visit"), None, None),
            P("patch", "visit", None),
            P(("patch", "visit")),
            P(("patch", "visit"), None),
            P(("patch", "visit")),
        ),
        out_specs=(P(("patch", "visit"), None, None), P("visit", None)),
        check_vma=False,
    )
```

profile of v0, /device:TPU:1, one launch (start us, length us, event | category | flops | bytes accessed | tf_op | source)
XLA Modules:
  0.0 1491.1 jit_solution(16165808198960752670)
XLA Ops:
  11.0 20.6 %all-to-all-start = ((s32[128,2,4]{2,1,0:T(2,128)}), s32[128,2,4]{2,1,0:T(2,128)S(1)}, u32[]{:S(2)}, u32[]{:S(2)}) async-start(s32[128,2,4]{2,1,0:T(2,128)} %copy.197), calls=%async_computation | async-start | bytes 262144 | tf_op jit(solution)/shard_map/all_to_all | solution.py:255
  33.5 2.1 broadcast_select_fusion.3
  35.7 11.7 all-to-all-done
  47.5 7.3 all-to-all-start.1
  54.7 11.8 all_gather.3
  67.0 3.7 all-to-all-done.1
  70.7 13.7 all-to-all-start.2
  84.4 668.7 %while.25 = (s32[]{:T(128)}, bf16[256,1024]{1,0:T(8,128)(2,1)S(1)}, s32[256,2]{0,1:T(2,128)S(1)}, bf16[256,22,148]{2,1,0:T(8,128)(2,1)}, s32[]{:T(128)}) while((s32[]{:T(128)}, bf16[256,1024]{1,0:T(8,128)(2,1)S(1)}, s32[256,2]{0,1:T(2,128)S(1)}, bf16[256,22,148]{2,1,0:T(8,128)(2,1)}, s32[]{:T(128)}) %tuple.139), condition=%wide.while_cond, body=%wide.while_body.sunk | while | flops 2 | bytes 20433 | solution.py:78
  108.6 2.0 bitcast_dynamic-update-slice_fusion.2
  111.2 2.0 bitcast_dynamic-update-slice_fusion.2
  124.3 2.0 bitcast_dynamic-update-slice_fusion.2
  134.7 2.0 bitcast_dynamic-update-slice_fusion.2
  140.0 2.0 bitcast_dynamic-update-slice_fusion.2
  147.8 2.0 bitcast_dynamic-update-slice_fusion.2
  160.9 2.0 bitcast_dynamic-update-slice_fusion.2
  163.5 2.0 bitcast_dynamic-update-slice_fusion.2
  174.0 2.0 bitcast_dynamic-update-slice_fusion.2
  181.8 2.0 bitcast_dynamic-update-slice_fusion.2
  194.9 2.0 bitcast_dynamic-update-slice_fusion.2
  205.3 2.0 bitcast_dynamic-update-slice_fusion.2
  234.0 2.0 bitcast_dynamic-update-slice_fusion.2
  299.3 2.0 bitcast_dynamic-update-slice_fusion.2
  330.7 2.0 bitcast_dynamic-update-slice_fusion.2
  349.0 2.0 bitcast_dynamic-update-slice_fusion.2
  403.8 2.0 bitcast_dynamic-update-slice_fusion.2
  440.4 2.0 bitcast_dynamic-update-slice_fusion.2
  466.5 2.0 bitcast_dynamic-update-slice_fusion.2
  487.4 2.0 bitcast_dynamic-update-slice_fusion.2
  500.4 2.0 bitcast_dynamic-update-slice_fusion.2
  529.2 2.0 bitcast_dynamic-update-slice_fusion.2
  537.0 2.0 bitcast_dynamic-update-slice_fusion.2
  542.2 2.0 bitcast_dynamic-update-slice_fusion.2
  550.1 2.0 bitcast_dynamic-update-slice_fusion.2
  581.4 2.0 bitcast_dynamic-update-slice_fusion.2
  591.9 2.0 bitcast_dynamic-update-slice_fusion.2
  612.8 2.0 bitcast_dynamic-update-slice_fusion.2
  636.3 2.0 bitcast_dynamic-update-slice_fusion.2
  662.4 2.0 bitcast_dynamic-update-slice_fusion.2
  683.3 2.0 bitcast_dynamic-update-slice_fusion.2
  738.1 2.0 bitcast_dynamic-update-slice_fusion.2
  753.3 66.2 %while.26 = (s32[]{:T(128)}, f32[8,16,28,28]{3,1,2,0:T(8,128)}, f32[8,16,28]{2,1,0:T(8,128)S(1)}, s32[8,32]{1,0:T(8,128)S(1)}, s32[8,32]{1,0:T(8,128)S(1)}, /*in...) while((s32[]{:T(128)}, f32[8,16,28,28]{3,1,2,0:T(8,128)}, ...), condition=%wide.region_4.7_spmd.clone, body=%wide.region_3.6_spmd.clone.sunk | while | flops 90732320 | bytes 13360773 | solution.py:155
  821.4 491.1 %all-reduce = (f32[16,28]{1,0:T(8,128)S(1)}, f32[16,28,28]{1,2,0:T(8,128)S(1)}) all-reduce(f32[16,28]{1,0:T(8,128)S(1)} %reduce_sum.270, f32[16,28,28]{1,2,0:T(8,128)S(1)} %copy.200), channel_id=1, replica_groups=mesh['patch'=128,'visit'=4] {'patch'}, use_global_device_ids=true, to_apply=%region_10.13 | all-reduce | flops 12992 | bytes 103936 | tf_op jit(solution)/shard_map/psum | solution.py:179
  1312.8 41.0 %custom-call.11 = f32[16,28,28]{2,1,0:T(8,128)S(1)} custom-call(f32[16,28,28]{2,1,0:T(8,128)S(1)} %fusion.103), custom_call_target="Cholesky" | custom-call | tf_op jit(solution)/shard_map/jit(cholesky)/cholesky | solution.py:180
  1354.1 34.5 %custom-call.12 = f32[16,1,28,28]{2,3,1,0:T(8,128)S(1)} custom-call(f32[16,1,28,28]{3,2,1,0:T(8,128)S(1)} %select_bitcast_fusion.2), custom_call_target="InvertDiagBlocksLowerTriangular" | custom-call | tf_op jit(solution)/shard_map/jit(_cho_solve)/vmap()/triangular_solve | solution.py:181
  1389.7 2.2 scatter_fusion
  1392.1 65.5 %while.27 = (s32[]{:T(128)}, bf16[8,32,2,128]{3,2,1,0:T(2,128)(2,1)}, s32[8,32]{1,0:T(8,128)S(1)}, f32[16,28]{0,1:T(8,128)S(1)}, f32[16,11,11]{2,1,0:T(8,128)S(1...) while((s32[]{:T(128)}, ...), condition=%wide.region_34.37_spmd.clone, body=%wide.region_12.36_spmd.clone.sunk | while | flops 22240096 | bytes 10662593 | solution.py:155
  1457.6 15.9 %all-to-all-start.3 = ((bf16[128,2,2,128]{3,2,1,0:T(2,128)(2,1)}), bf16[128,2,2,128]{3,2,1,0:T(2,128)(2,1)S(1)}, u32[]{:S(2)}, u32[]{:S(2)}) async-start(bf16[128,2,2,128]{3,2,1,0:T(2,128)(2,1)} %bitcast.21), calls=%async_computation.3 | async-start | bytes 262144 | tf_op jit(solution)/shard_map/all_to_all | solution.py:276
  1473.5 16.0 %all-to-all-done.3 = bf16[128,2,2,128]{3,2,1,0:T(2,128)(2,1)S(1)} async-done(((bf16[128,2,2,128]{3,2,1,0:T(2,128)(2,1)}), bf16[128,2,2,128]{3,2,1,0:T(2,128)(2,1)S(1)}, u32[]{:S(2)}, u32[]{:S(2)}) %all-to-all-start.3) | async-done | bytes 131104 | tf_op jit(solution)/shard_map/all_to_all | solution.py:276
  (1289 shorter events, 752.5 us)
Async XLA Ops:
  0.6 2.1 copy-start
  0.6 35.1 %copy-start.8 = (bf16[21,11]{1,0:T(8,128)(2,1)S(1)}, bf16[21,11]{1,0:T(8,128)(2,1)}, u32[]{:S(2)}) copy-start(bf16[21,11]{1,0:T(8,128)(2,1)} %constant.213) | copy-start | bytes 1390
  0.7 30.9 %copy-start.4 = (f32[128,2,128]{2,1,0:T(2,128)S(1)}, f32[128,2,128]{2,1,0:T(2,128)}, u32[]{:S(2)}) copy-start(f32[128,2,128]{2,1,0:T(2,128)} %param.19) | copy-start | bytes 393220
  0.7 30.9 %copy-start.6 = (f32[128,2,128]{2,1,0:T(2,128)S(1)}, f32[128,2,128]{2,1,0:T(2,128)}, u32[]{:S(2)}) copy-start(f32[128,2,128]{2,1,0:T(2,128)} %param.20) | copy-start | bytes 393220
  0.7 35.0 %copy-start.5 = (f32[1,64,1024]{2,1,0:T(8,128)S(1)}, f32[1,64,1024]{2,1,0:T(8,128)}, u32[]{:S(2)}) copy-start(f32[1,64,1024]{2,1,0:T(8,128)} %param.21) | copy-start | bytes 786436
  7.2 746.1 %copy-start.1 = (bf16[11,148,128]{2,1,0:T(8,128)(2,1)S(1)}, bf16[11,148,128]{2,1,0:T(8,128)(2,1)}, u32[]{:S(2)}) copy-start(bf16[11,148,128]{2,1,0:T(8,128)(2,1)} %constant.203) | copy-start | bytes 1250308
  7.2 746.1 %copy-start.2 = (bf16[22,22,1]{1,0,2:T(8,128)(2,1)S(1)}, bf16[22,22,1]{1,0,2:T(8,128)(2,1)}, u32[]{:S(2)}) copy-start(bf16[22,22,1]{1,0,2:T(8,128)(2,1)} %constant.404) | copy-start | bytes 2908
  11.0 36.5 %all-to-all-start = ((s32[128,2,4]{2,1,0:T(2,128)}), s32[128,2,4]{2,1,0:T(2,128)S(1)}, u32[]{:S(2)}, u32[]{:S(2)}) async-start(s32[128,2,4]{2,1,0:T(2,128)} %copy.197), calls=%async_computation | async-start | bytes 262144 | tf_op jit(solution)/shard_map/all_to_all | solution.py:255
  47.5 23.2 %all-to-all-start.1 = ((bf16[128,2,2,128]{3,2,1,0:T(2,128)(2,1)}), bf16[128,2,2,128]{3,2,1,0:T(2,128)(2,1)S(1)}, u32[]{:S(2)}, u32[]{:S(2)}) async-start(bf16[128,2,2,128]{3,2,1,0:T(2,128)(2,1)} %bitcast.5), calls=%async_computation.1 | async-start | bytes 262144 | tf_op jit(solution)/shard_map/all_to_all | solution.py:248
  70.7 682.6 %all-to-all-start.2 = ((bf16[128,2,2,128]{3,2,1,0:T(2,128)(2,1)}), bf16[128,2,2,128]{3,2,1,0:T(2,128)(2,1)S(1)}, u32[]{:S(2)}, u32[]{:S(2)}) async-start(bf16[128,2,2,128]{3,2,1,0:T(2,128)(2,1)} %bitcast.7), calls=%async_computation.2 | async-start | bytes 262144 | tf_op jit(solution)/shard_map/all_to_all | solution.py:241
  819.5 570.2 %copy-start.3 = (s32[27]{0:T(128)S(1)}, s32[27]{0:T(128)}, u32[]{:S(2)}) copy-start(s32[27]{0:T(128)} %constant.241) | copy-start | bytes 328
  1389.5 2.5 copy-start.7
  1457.6 31.9 %all-to-all-start.3 = ((bf16[128,2,2,128]{3,2,1,0:T(2,128)(2,1)}), bf16[128,2,2,128]{3,2,1,0:T(2,128)(2,1)S(1)}, u32[]{:S(2)}, u32[]{:S(2)}) async-start(bf16[128,2,2,128]{3,2,1,0:T(2,128)(2,1)} %bitcast.21), calls=%async_computation.3 | async-start | bytes 262144 | tf_op jit(solution)/shard_map/all_to_all | solution.py:276
where the time goes:
time: 1500 us; the launch traced here: 1490 us
  local copies, waits for them, and re-layouts  718 us (48%)
  blocking collectives  503 us (34%)
  other arithmetic  122 us (8%)
  starting transfers between devices  57.4 us (4%)
  matrix products  54.7 us (4%)
  waiting for transfers between devices  31.4 us (2%)
    gather x768, local copies, waits for them, and re-layouts  668 us
    psum x1, blocking collectives, fit_coefficients(): gram_total, right_total = lax.psum((gram_total, right_total), 'patch')  491 us
    another operation x4, other arithmetic, fit_coefficients(): factor = jnp.linalg.cholesky(gram_total)  41.2 us
    another operation x3, other arithmetic, fit_coefficients(): jax.scipy.linalg.cho_solve((factor, True), right_total[..., None])[..., 0]  34.6 us
    reduce_sum x24, other arithmetic, model_block(): model = model + jnp.sum(weighted, axis=1)  31.4 us
  transfers between devices with their start and end apart: 4, of which 3 were waited for; matrix products, arithmetic and copies ran while one was open for 45% of the time, Pallas kernels for 0%

commit v1 on v0

v1 whole, which is shorter than its diff:
```python
import functools

import jax
import jax.numpy as jnp
import numpy as np
from jax import lax
from jax.experimental import pallas as pl
from jax.experimental.pallas import tpu as pltpu
from jax.sharding import PartitionSpec as P

KR = 10
TAPS = 2 * KR + 1
NB = 28
VIS_DEV = 16
ROWS = 32
LANES = 128
GROUP = 8
SLOT_ROWS = 10

gauss_widths = (1.0, 2.0, 4.0)
poly_degrees = (4, 2, 2)

SET_P = (0, 1, 2, 3, 4, 5, 6, 7)
SET_Q = (8, 9, 10, 0, 1, 0, 8, 9)
COLS_P = (0, 1, 2, 5, 6, 7)
COLS_Q = (8, 3, 4, 9, 10)

ROW_PAIRS = (
    [(0, b) for b in range(5)] + [(5, 5), (5, 6), (5, 7)]
    + [(1, b) for b in range(4)] + [None, (6, 5), (6, 6), None]
    + [(2, 0), (2, 1), (2, 2), None, None, (7, 5), (10, 8), None]
    + [(8, 8), (8, 9), (8, 10), (3, 0), (3, 1), (4, 0), (9, 8), (9, 9)]
)
WEIGHT_ROW = 12
SCIENCE_ROW = 15


def filter_table(radius):
    tap_points = np.arange(-radius, radius + 1) * 1.0
    raw_columns = []
    for width_value, degree in zip(gauss_widths, poly_degrees):
        bell_curve = np.exp(-tap_points * tap_points / (2.0 * width_value * width_value))
        for power_index in range(degree + 1):
            raw_columns.append(bell_curve * (tap_points / radius) ** power_index)
    orthonormal = []
    for column in raw_columns:
        vector = column.copy()
        for repeat_index in range(2):
            for earlier in orthonormal:
                vector = vector - np.dot(earlier, vector) * earlier
        orthonormal.append(vector / np.sqrt(np.dot(vector, vector)))
    return np.stack(orthonormal, axis=1).astype(np.float32)


def basis_rows():
    rows = []
    offset = 0
    for degree in poly_degrees:
        for first in range(degree + 1):
            for second in range(degree + 1 - first):
                rows.append(ROW_PAIRS.index((offset + first, offset + second)))
        offset += degree + 1
    return rows + [WEIGHT_ROW]


def constants():
    values = filter_table(KR)
    band = np.zeros((256, 48), np.float32)
    for which, held in enumerate((SET_P, SET_Q)):
        for y in range(16):
            for row, b in enumerate(held):
                band[which * 128 + y * 8 + row, y : y + TAPS] = values[:, b]
    columns = []
    for held in (COLS_P, COLS_Q):
        wide = np.zeros((256, len(held) * LANES), np.float32)
        for place, a in enumerate(held):
            for j in range(LANES):
                wide[j : j + TAPS, place * LANES + j] = values[:, a]
        columns.append(wide)
    return [jnp.asarray(c).astype(jnp.bfloat16) for c in (band, *columns)]


def iota(shape, axis):
    return lax.broadcasted_iota(jnp.int32, shape, axis)


def pack_kernel(science, sigma, dest, visit, offsets, packed, slots, stack):
    d = jnp.broadcast_to(dest[...], (LANES, LANES))
    earlier = (d.T == d) & (iota(d.shape, 0) < iota(d.shape, 1))
    rank = jnp.sum(jnp.where(earlier, 1, 0), axis=0, keepdims=True)
    slots[...] = jnp.broadcast_to(dest[...] * 2 + rank, slots.shape)
    for i in range(2):
        weight = sigma[pl.ds(i, LANES, stride=2), :]
        scaled = science[pl.ds(i, LANES, stride=2), :] * weight
        stack[i * LANES : (i + 1) * LANES, :] = scaled.astype(jnp.bfloat16)
        stack[(2 + i) * LANES : (3 + i) * LANES, :] = weight.astype(jnp.bfloat16)
    column = offsets[1:2, :]
    fields = (visit[...], offsets[0:1, :], column >> 7, column & 127)
    row = iota((LANES, LANES), 0)
    details = jnp.zeros((LANES, LANES), jnp.float32)
    for place, field in enumerate(fields):
        details = jnp.where(row == place, field.astype(jnp.float32), details)
    stack[4 * LANES :, :] = details.T.astype(jnp.bfloat16)
    first = dest[...] * SLOT_ROWS
    targets = (first + 2 * rank, first + 2 * rank + 1, first + 4 + 2 * rank,
               first + 5 + 2 * rank, first + 8 + rank)
    target = jnp.concatenate(targets, axis=1)
    block = 256
    for start in range(0, packed.shape[0], block):
        chosen = iota((block, 5 * LANES), 0) + start == target
        chosen = jnp.where(chosen, 1.0, 0.0).astype(jnp.bfloat16)
        packed[start : start + block, :] = jnp.dot(
            chosen, stack[...], preferred_element_type=jnp.float32
        ).astype(jnp.bfloat16)


def fit_kernel(arrived, template, band, wide_p, wide_q, images, gram, details_out,
               rows_p, rows_q, data, left_p, left_q, right_p, right_q, design,
               total, details, sem):
    data[...] = arrived[...].astype(jnp.float32)
    for c in range(2):
        fields = data[pl.ds(8 + c, LANES, stride=SLOT_ROWS), :].T
        details_out[c] = fields[0:8, :].astype(jnp.int32)
    copy = pltpu.make_async_copy(details_out, details, sem)
    copy.start()
    for y in range(0, 240, 16):
        depth = min(48, 256 - y)
        made = jnp.dot(band[:, 0:depth], template[y : y + depth, :],
                       preferred_element_type=jnp.float32)
        made = made.astype(jnp.bfloat16).astype(jnp.float32)
        rows_p[y * 8 : y * 8 + 128, :] = made[0:128]
        rows_q[y * 8 : y * 8 + 128, :] = made[128:256]
    total[...] = jnp.zeros_like(total)
    copy.wait()
    lane = iota((16, LANES), 1)
    sub = iota((8, LANES), 0)
    quarter = iota((ROWS, LANES), 1) >> 5

    def step(g, carry):
        for t in range(GROUP):
            c = t % 2
            src = g * (GROUP // 2) + t // 2
            r = details[c, 1, src]
            q = details[c, 2, src]
            s = details[c, 3, src]
            back = (LANES - s) & 127
            keep = lane < LANES - s
            for rows, left in ((rows_p, left_p), (rows_q, left_q)):
                turned = []
                for m in range(3):
                    at = pl.multiple_of(jnp.minimum(q + m, 7) * LANES, LANES)
                    piece = rows[pl.ds(pl.multiple_of(r * 8, 8), 16), pl.ds(at, LANES)]
                    turned.append(pltpu.roll(piece, back, 1))
                for m in range(2):
                    left[t * 16 : t * 16 + 16, m * LANES : (m + 1) * LANES] = jnp.where(
                        keep, turned[m], turned[m + 1]
                    ).astype(jnp.bfloat16)
        right_p[...] = jnp.dot(left_p[...], wide_p[...], preferred_element_type=jnp.float32)
        right_q[...] = jnp.dot(left_q[...], wide_q[...], preferred_element_type=jnp.float32)
        for t in range(GROUP):
            c = t % 2
            src = g * (GROUP // 2) + t // 2
            for i in range(2):
                at = t * 16 + i * 8

                def p(a):
                    k = COLS_P.index(a)
                    return right_p[at : at + 8, k * LANES : (k + 1) * LANES]

                def q(a):
                    k = COLS_Q.index(a)
                    return right_q[at : at + 8, k * LANES : (k + 1) * LANES]

                v0 = jnp.where(sub < 5, p(0), p(5))
                v1 = jnp.where(sub < 4, p(1), jnp.where(sub == 7, 0.0, p(6)))
                v1 = jnp.where(sub == 4, 1.0, v1)
                v2 = jnp.where(sub < 3, p(2), jnp.where(sub == 5, p(7), jnp.where(sub == 6, q(10), 0.0)))
                v3 = jnp.where(sub < 3, q(8), jnp.where(sub < 5, q(3), jnp.where(sub < 6, q(4), q(9))))
                lanes = slice(i * LANES, (i + 1) * LANES)
                first = pl.multiple_of((g * GROUP + t) * ROWS, ROWS)
                for m, v in enumerate((v0, v1, v2, v3)):
                    images[pl.ds(first + 8 * m, 8), lanes] = v
                weight = data[pl.ds(src * SLOT_ROWS + 4 + 2 * c + i, 1), :]
                science = data[pl.ds(src * SLOT_ROWS + 2 * c + i, 1), :]
                d1 = jnp.where(sub == 7, science, v1 * weight)
                whole = jnp.concatenate([v0 * weight, d1, v2 * weight, v3 * weight], axis=0)
                design[t * ROWS : (t + 1) * ROWS, lanes] = whole.astype(jnp.bfloat16)
        for h in range(GROUP // 4):
            part = design[h * 128 : (h + 1) * 128, :]
            product = lax.dot_general(part, part, (((1,), (1,)), ((), ())),
                                      preferred_element_type=jnp.float32)
            for n in range(4):
                t = h * 4 + n
                v = details[t % 2, 0, g * (GROUP // 2) + t // 2]
                total[v] += jnp.where(quarter == n, product[n * ROWS : (n + 1) * ROWS, :], 0.0)
        return carry

    lax.fori_loop(0, 2 * LANES // GROUP, step, 0)
    lane8 = iota((8, LANES), 1) >> 5
    for v in range(VIS_DEV):
        whole = total[v]
        whole = whole + pltpu.roll(whole, 64, 1)
        whole = whole + pltpu.roll(whole, 32, 1)
        low = jnp.where(lane8 == 0, whole[0:8], whole[8:16])
        high = jnp.where(lane8 == 2, whole[16:24], whole[24:32])
        gram[v * 8 : v * 8 + 8, :] = jnp.where(lane8 < 2, low, high)


def middle_kernel(parts, out):
    whole = parts[0]
    for n in range(1, parts.shape[0]):
        whole = whole + parts[n]
    for n in range(out.shape[0]):
        out[n] = whole


def solve_kernel(parts, out):
    whole = parts[0]
    for n in range(1, parts.shape[0]):
        whole = whole + parts[n]
    lane8 = iota((8, LANES), 1) >> 5
    pieces = []
    for p in range(4):
        piece = jnp.zeros((8, LANES), jnp.float32)
        for h in range(2):
            turned = whole[h * 8 : h * 8 + 8]
            shift = (32 * h - 32 * p) % LANES
            if shift:
                turned = pltpu.roll(turned, shift, 1)
            piece = jnp.where(lane8 == h, turned, piece)
        pieces.append(piece)
    matrix = jnp.concatenate(pieces, axis=0)
    lane = iota((ROWS, LANES), 1)
    row_lane = iota((1, LANES), 1)
    half = lane < 32
    for k in basis_rows():
        row = matrix[k : k + 1, :]
        column = jnp.where(half, matrix[:, k : k + 1], matrix[:, 32 + k : 33 + k])
        pivot = jnp.broadcast_to(column[k : k + 1, :], (ROWS, LANES))
        scaled = column / pivot
        matrix = jnp.where((lane & 31) == k, scaled, matrix - scaled * row)
    answer = matrix[SCIENCE_ROW : SCIENCE_ROW + 1, :]
    valid = row_lane < 0
    for k in basis_rows():
        valid = valid | ((row_lane & 31) == k)
    answer = jnp.where(valid & (row_lane < 64), answer, 0.0)
    for n in range(out.shape[0]):
        out[n] = answer


def model_kernel(details, answers, images, model, wide, sums):
    block = images.shape[0] // ROWS
    g = pl.program_id(0)

    @pl.when(g == 0)
    def _():
        turned = jnp.concatenate([answers[...], jnp.zeros((LANES - 8, LANES), jnp.float32)], axis=0).T
        for v in range(VIS_DEV):
            piece = turned[(v % 2) * ROWS : (v % 2) * ROWS + ROWS, v // 2 : v // 2 + 1]
            wide[v] = jnp.broadcast_to(piece, (ROWS, LANES))

    for t in range(block):
        v = details[t % 2, 0, g * (block // 2) + t // 2]
        for i in range(2):
            lanes = slice(i * LANES, (i + 1) * LANES)
            acc = wide[v, 0:8] * images[t * ROWS : t * ROWS + 8, lanes]
            for m in range(1, 4):
                acc = acc + wide[v, 8 * m : 8 * m + 8] * images[t * ROWS + 8 * m : t * ROWS + 8 * m + 8, lanes]
            sums[(2 * t + i) * 8 : (2 * t + i) * 8 + 8, :] = acc
    out = sums[pl.ds(0, 2 * block, stride=8), :]
    for n in range(1, 8):
        out = out + sums[pl.ds(n, 2 * block, stride=8), :]
    model[...] = out.astype(jnp.bfloat16)


def final_kernel(slots, science, returned, out):
    column = jnp.broadcast_to(slots[0:1, :], (LANES, LANES)).T
    column = jnp.concatenate([column] * 4, axis=1)
    for i in range(2):
        chosen = iota((LANES, 4 * LANES), 1) == column * 2 + i
        chosen = jnp.where(chosen, 1.0, 0.0).astype(jnp.bfloat16)
        model = jnp.dot(chosen, returned[...], preferred_element_type=jnp.float32)
        out[pl.ds(i, LANES, stride=2), :] = science[pl.ds(i, LANES, stride=2), :] - model


def vmem(count):
    return [pl.BlockSpec(memory_space=pltpu.VMEM)] * count


def shape(dims, dtype=jnp.float32):
    return jax.ShapeDtypeStruct(dims, dtype)


def params(**more):
    return pltpu.CompilerParams(vmem_limit_bytes=60 << 20, **more)


def pack(science, sigma, dest, visit, offsets):
    return pl.pallas_call(
        pack_kernel,
        out_shape=(shape((LANES * SLOT_ROWS, LANES), jnp.bfloat16), shape((8, LANES), jnp.int32)),
        in_specs=vmem(5), out_specs=tuple(vmem(2)),
        scratch_shapes=[pltpu.VMEM((5 * LANES, LANES), jnp.bfloat16)],
        compiler_params=params(), name="pack",
    )(science, sigma, dest, visit, offsets)


def fit(arrived, template, band, wide_p, wide_q):
    return pl.pallas_call(
        fit_kernel,
        out_shape=(shape((2 * LANES * ROWS, 2 * LANES)), shape((VIS_DEV * 8, LANES)),
                   shape((2, 8, LANES), jnp.int32)),
        in_specs=vmem(5), out_specs=tuple(vmem(3)),
        scratch_shapes=[
            pltpu.VMEM((1920, 1024), jnp.float32), pltpu.VMEM((1920, 1024), jnp.float32),
            pltpu.VMEM((LANES * SLOT_ROWS, LANES), jnp.float32),
            pltpu.VMEM((GROUP * 16, 256), jnp.bfloat16), pltpu.VMEM((GROUP * 16, 256), jnp.bfloat16),
            pltpu.VMEM((GROUP * 16, len(COLS_P) * LANES), jnp.float32),
            pltpu.VMEM((GROUP * 16, len(COLS_Q) * LANES), jnp.float32),
            pltpu.VMEM((GROUP * ROWS, 256), jnp.bfloat16),
            pltpu.VMEM((VIS_DEV, ROWS, LANES), jnp.float32),
            pltpu.SMEM((2, 8, LANES), jnp.int32), pltpu.SemaphoreType.DMA,
        ],
        compiler_params=params(), name="fit",
    )(arrived, template, band, wide_p, wide_q)


def middle(parts):
    return pl.pallas_call(middle_kernel, out_shape=shape((16,) + parts.shape[1:]),
                          in_specs=vmem(1), out_specs=vmem(1)[0], name="middle")(parts)


def solve(parts):
    return pl.pallas_call(solve_kernel, out_shape=shape((8, 1, LANES)),
                          in_specs=vmem(1), out_specs=vmem(1)[0], name="solve")(parts)


def model_of(details, answers, images):
    block = 32
    return pl.pallas_call(
        model_kernel,
        out_shape=shape((4 * LANES, LANES), jnp.bfloat16),
        grid=(2 * LANES // block,),
        in_specs=[pl.BlockSpec(memory_space=pltpu.SMEM),
                  pl.BlockSpec((8, LANES), lambda g: (0, 0)),
                  pl.BlockSpec((block * ROWS, 2 * LANES), lambda g: (g, 0))],
        out_specs=pl.BlockSpec((2 * block, LANES), lambda g: (g, 0)),
        scratch_shapes=[pltpu.VMEM((VIS_DEV, ROWS, LANES), jnp.float32),
                        pltpu.VMEM((block * 16, LANES), jnp.float32)],
        compiler_params=params(), name="model",
    )(details, answers, images)


def final(slots, science, returned):
    return pl.pallas_call(final_kernel, out_shape=shape((2 * LANES, LANES)),
                          in_specs=vmem(3), out_specs=vmem(1)[0], name="final")(slots, science, returned)


def exchange(values, groups=None):
    return lax.all_to_all(values, "patch", split_axis=0, concat_axis=0, tiled=True,
                          axis_index_groups=groups)


def per_device(science, inverse_sigma, template, destination, offsets, visit_local):
    patches = lax.axis_size("patch")
    planes = [[z * 8 + i for i in range(8)] for z in range(patches // 8)]
    lines = [[z * 8 + i for z in range(patches // 8)] for i in range(8)]
    band, wide_p, wide_q = constants()
    whole_template = lax.all_gather(template[0].astype(jnp.bfloat16), "visit", axis=0, tiled=True)
    science_rows = science.reshape(2 * LANES, LANES)
    packed, slots = pack(science_rows, inverse_sigma.reshape(2 * LANES, LANES),
                         destination.reshape(1, LANES), visit_local.reshape(1, LANES), offsets.T)
    arrived = exchange(packed.reshape(patches, 5, 2, LANES)).reshape(LANES * SLOT_ROWS, LANES)
    images, gram, details = fit(arrived, whole_template, band, wide_p, wide_q)
    parts = exchange(gram.reshape(8, 16, LANES), planes)
    parts = exchange(middle(parts), lines)
    answers = exchange(solve(parts), planes).reshape(8, LANES)
    model = model_of(details, answers, images)
    returned = exchange(model.reshape(patches, 2, 2, LANES)).reshape(4 * LANES, LANES)
    difference = final(slots, science_rows, returned)
    table = jnp.concatenate([answers[:, 0:32], answers[:, 32:64]], axis=1).reshape(VIS_DEV, ROWS)
    coefficients = jnp.stack([table[:, k] for k in basis_rows()], axis=1)
    return difference.reshape(science.shape), coefficients


def solution(mesh):
    return jax.shard_map(
        per_device,
        mesh=mesh,
        in_specs=(
            P(("patch", "visit"), None, None),
            P(("patch", "visit"), None, None),
            P("patch", "visit", None),
            P(("patch", "visit")),
            P(("patch", "visit"), None),
            P(("patch", "visit")),
        ),
        out_specs=(P(("patch", "visit"), None, None), P("visit", None)),
        check_vma=False,
    )
```

time: 1500 us -> 152 us (0.10)
  local copies, waits for them, and re-layouts: 718 us -> 2.98 us
  blocking collectives: 503 us -> 51.1 us
  other arithmetic: 122 us -> 0.97 us
  matrix products: 54.7 us -> 0 us
  Pallas kernels: 0 us -> 43.5 us
  starting transfers between devices: 57.4 us -> 26.9 us
    gather x790 -> x0, local copies, waits for them, and re-layouts: 687 us -> none
    psum x1 -> x0, blocking collectives: 491 us -> none  [fit_coefficients(): gram_total, right_total = lax.psum((gram_total, right_total), 'patch')]
    another operation x7 -> x0, other arithmetic: 75.8 us -> none  [the longest x4 41.2 us: fit_coefficients(): factor = jnp.linalg.cholesky(gram_total)]
    dot_general x144 -> x0, matrix products: 53.8 us -> none  [the longest x16 20.1 us: filtered_block(): jnp.einsum('ry,nyx->nrx', row_matrix, windows, preferred_element_type=jnp...]
    pallas_call x0 -> x6, Pallas kernels: none -> 43.5 us  [the longest x1 26.6 us: fit(): pl.pallas_call(fit_kernel, out_shape=(shape((2 * LANES * ROWS, 2 * LANES)...]
    all_to_all x0 -> x3, blocking collectives: none -> 39 us  [exchange(): lax.all_to_all(values, 'patch', split_axis=0, concat_axis=0, tiled=True,...]
    reduce_sum x28 -> x0, other arithmetic: 34.1 us -> none  [the longest x24 31.4 us: model_block(): model = model + jnp.sum(weighted, axis=1)]
    all_to_all x4 -> x2, starting transfers between devices: 57.4 us -> 26.9 us  [exchange(): lax.all_to_all(values, 'patch', split_axis=0, concat_axis=0, tiled=True,...]
  transfers between devices with their start and end apart: 4 -> 2, of which waited for: 3 -> 2; matrix products, arithmetic and copies ran while one was open for 45% -> 1% of each run, Pallas kernels for 0% -> 0%
where the time goes in v1:
time: 152 us; the launch traced here: 151 us
  blocking collectives  51.1 us (34%)
  Pallas kernels  43.5 us (29%)
  starting transfers between devices  26.9 us (18%)
  waiting for transfers between devices  24.6 us (16%)
  local copies, waits for them, and re-layouts  2.98 us (2%)
    all_to_all x3, blocking collectives, exchange(): lax.all_to_all(values, 'patch', split_axis=0, concat_axis=0, tiled=True,...  39 us
    all_to_all x2, starting transfers between devices, exchange(): lax.all_to_all(values, 'patch', split_axis=0, concat_axis=0, tiled=True,...  26.9 us
    pallas_call x1, Pallas kernels, fit(): pl.pallas_call(fit_kernel, out_shape=(shape((2 * LANES * ROWS, 2 * LANES)...  26.6 us
    all_to_all x2, waiting for transfers between devices, exchange(): lax.all_to_all(values, 'patch', split_axis=0, concat_axis=0, tiled=True,...  24.6 us
    all_gather x1, blocking collectives, per_device(): lax.all_gather(template[0].astype(jnp.bfloat16), 'visit', axis=0, tiled=T...  12.1 us
    pallas_call x1, Pallas kernels, model_of(): pl.pallas_call(model_kernel, out_shape=shape((4 * LANES, LANES), jnp.bflo...  7.09 us
    pallas_call x1, Pallas kernels, solve(): pl.pallas_call(solve_kernel, out_shape=shape((8, 1, LANES)), in_specs=vme...  3.97 us
  transfers between devices with their start and end apart: 2, of which 2 were waited for; matrix products, arithmetic and copies ran while one was open for 1% of the time, Pallas kernels for 0%

profile of v1, /device:TPU:1, one launch (start us, length us, event | category | flops | bytes accessed | tf_op | source)
XLA Modules:
  0.0 150.8 jit_solution(13187679215403784407)
XLA Ops:
  0.6 2.5 %pack.1 = (bf16[1280,128]{1,0:T(8,128)(2,1)}, s32[8,128]{1,0:T(8,128)}) custom-call(f32[256,128]{1,0:T(8,128)} %bitcast.19, f32[256,128]{1,0:T(8,128)} %bitcast.24, s32[1,128]{1,0:T(1,128)} %bitcast.29, s32[1,128]{1,0:T(1,128)} %bitcast.30, s32[2,128]{1,0:T(2,128)} %bitcast.28), custom_call_target="tpu_custom_call" | custom-call | tf_op jit(solution)/shard_map/pack/pallas_call | solution.py:299
  3.1 20.6 %all-to-all-start = ((bf16[128,5,2,128]{3,2,1,0:T(2,128)(2,1)}), bf16[128,5,2,128]{3,2,1,0:T(2,128)(2,1)S(1)}, u32[]{:S(2)}, u32[]{:S(2)}) async-start(bf16[128,5,2,128]{3,2,1,0:T(2,128)(2,1)} %bitcast.22), calls=%async_computation | async-start | bytes 655360 | tf_op jit(solution)/shard_map/all_to_all | solution.py:360
  23.6 1.0 convert_element_type.15
  24.6 12.1 %all-gather = bf16[1,256,1024]{2,1,0:T(8,128)(2,1)} all-gather(bf16[1,64,1024]{2,1,0:T(8,128)(2,1)S(1)} %convert_element_type.15), channel_id=2, replica_groups=mesh['patch'=128,'visit'=4] {'visit'}, dimensions={1}, use_global_device_ids=true | all-gather | bytes 655360 | tf_op jit(solution)/shard_map/all_gather | solution.py:369
  36.7 9.6 %all-to-all-done = bf16[128,5,2,128]{3,2,1,0:T(2,128)(2,1)S(1)} async-done(((bf16[128,5,2,128]{3,2,1,0:T(2,128)(2,1)}), bf16[128,5,2,128]{3,2,1,0:T(2,128)(2,1)S(1)}, u32[]{:S(2)}, u32[]{:S(2)}) %all-to-all-start) | async-done | bytes 327712 | tf_op jit(solution)/shard_map/all_to_all | solution.py:360
  46.4 0.0 copy-start
  46.4 0.8 copy-done
  47.1 26.6 %fit.1 = (f32[8192,256]{1,0:T(8,128)}, f32[128,128]{1,0:T(8,128)}, s32[2,8,128]{2,1,0:T(8,128)}) custom-call(bf16[1280,128]{1,0:T(8,128)(2,1)} %bitcast.16, bf16[256,1024]{1,0:T(8,128)(2,1)} %bitcast.15, bf16[256,48]{1,0:T(8,128)(2,1)} %constant.15.band, bf16[256,768]{1,0:T(8,128)(2,1)} %constant.16.wide_p, bf16[256,640]{1,0:T(8,128)(2,1)} %constant.17.wide_q), custom_call_target="tpu_custom_call" | custom-call | tf_op jit(solution)/shard_map/fit/pallas_call | solution.py:309
  73.7 11.5 %all_to_all.25.parts = f32[8,16,128]{2,1,0:T(8,128)} all-to-all(f32[8,16,128]{2,1,0:T(8,128)} %bitcast.25), channel_id=1, replica_groups={{0,4,8,12,16,20,24,28},{32,36,40,44,48,52,56,60},{64,68,72,76,80,84,88,..., dimensions={0} | all-to-all | bytes 131072 | tf_op jit(solution)/shard_map/all_to_all | solution.py:360
  85.2 1.5 %middle.1 = f32[16,16,128]{2,1,0:T(8,128)} custom-call(f32[8,16,128]{2,1,0:T(8,128)} %all_to_all.25.parts), custom_call_target="tpu_custom_call" | custom-call | tf_op jit(solution)/shard_map/middle/pallas_call | solution.py:329
  86.7 16.1 %all_to_all.26.parts = f32[16,16,128]{2,1,0:T(8,128)} all-to-all(f32[16,16,128]{2,1,0:T(8,128)} %middle.1), channel_id=1, replica_groups={{0,32,64,96,128,160,192,224,256,288,320,352,384,416,448,480},{4,36,68,1..., dimensions={0} | all-to-all | bytes 262144 | tf_op jit(solution)/shard_map/all_to_all | solution.py:360
  102.8 4.0 %solve.1 = f32[8,1,128]{2,1,0:T(1,128)} custom-call(f32[16,16,128]{2,1,0:T(8,128)} %all_to_all.26.parts), custom_call_target="tpu_custom_call" | custom-call | tf_op jit(solution)/shard_map/solve/pallas_call | solution.py:334
  106.8 11.4 %all_to_all.27 = f32[8,1,128]{2,1,0:T(1,128)S(1)} all-to-all(f32[8,1,128]{2,1,0:T(1,128)} %solve.1), channel_id=1, replica_groups={{0,4,8,12,16,20,24,28},{32,36,40,44,48,52,56,60},{64,68,72,76,80,84,88,..., dimensions={0} | all-to-all | bytes 8192 | tf_op jit(solution)/shard_map/all_to_all | solution.py:360
  118.2 0.0 copy-start.2
  118.2 0.1 reshape.52
  118.3 0.5 copy-done.2
  118.8 7.1 %model.1 = bf16[512,128]{1,0:T(8,128)(2,1)} custom-call(s32[2,8,128]{2,1,0:T(8,128)} %get-tuple-element.9.details, f32[8,128]{1,0:T(8,128)} %bitcast.27, f32[8192,256]{1,0:T(8,128)} %get-tuple-element.11.images), custom_call_target="tpu_custom_call" | custom-call | tf_op jit(solution)/shard_map/model/pallas_call | solution.py:340
  125.9 6.4 %all-to-all-start.4 = ((bf16[128,2,2,128]{3,2,1,0:T(2,128)(2,1)}), bf16[128,2,2,128]{3,2,1,0:T(2,128)(2,1)S(1)}, u32[]{:S(2)}, u32[]{:S(2)}) async-start(bf16[128,2,2,128]{3,2,1,0:T(2,128)(2,1)} %bitcast.18), calls=%async_computation.4 | async-start | bytes 262144 | tf_op jit(solution)/shard_map/all_to_all | solution.py:360
  132.3 0.1 fusion.1
  132.3 0.1 slice.73
  132.4 0.1 fusion
  132.5 0.1 fusion.2
  132.6 0.7 stack.4
  133.3 15.0 %all-to-all-done.4 = bf16[128,2,2,128]{3,2,1,0:T(2,128)(2,1)S(1)} async-done(((bf16[128,2,2,128]{3,2,1,0:T(2,128)(2,1)}), bf16[128,2,2,128]{3,2,1,0:T(2,128)(2,1)S(1)}, u32[]{:S(2)}, u32[]{:S(2)}) %all-to-all-start.4) | async-done | bytes 131104 | tf_op jit(solution)/shard_map/all_to_all | solution.py:360
  148.3 0.0 copy-start.1
  148.3 0.6 copy-done.1
  148.9 1.9 %final.1 = f32[256,128]{1,0:T(8,128)} custom-call(s32[8,128]{1,0:T(8,128)} %get-tuple-element.7.slots, f32[256,128]{1,0:T(8,128)} %bitcast.20, bf16[512,128]{1,0:T(8,128)(2,1)} %bitcast.21), custom_call_target="tpu_custom_call" | custom-call | tf_op jit(solution)/shard_map/final/pallas_call | solution.py:355
Async XLA Ops:
  3.1 43.3 %all-to-all-start = ((bf16[128,5,2,128]{3,2,1,0:T(2,128)(2,1)}), bf16[128,5,2,128]{3,2,1,0:T(2,128)(2,1)S(1)}, u32[]{:S(2)}, u32[]{:S(2)}) async-start(bf16[128,5,2,128]{3,2,1,0:T(2,128)(2,1)} %bitcast.22), calls=%async_computation | async-start | bytes 655360 | tf_op jit(solution)/shard_map/all_to_all | solution.py:360
  46.4 0.8 copy-start
  118.2 0.6 copy-start.2
  125.9 22.4 %all-to-all-start.4 = ((bf16[128,2,2,128]{3,2,1,0:T(2,128)(2,1)}), bf16[128,2,2,128]{3,2,1,0:T(2,128)(2,1)S(1)}, u32[]{:S(2)}, u32[]{:S(2)}) async-start(bf16[128,2,2,128]{3,2,1,0:T(2,128)(2,1)} %bitcast.18), calls=%async_computation.4 | async-start | bytes 262144 | tf_op jit(solution)/shard_map/all_to_all | solution.py:360
  148.3 0.6 copy-start.1

commit v2 on v1

--- a/solution.py
+++ b/solution.py
@@ -14,7 +14,11 @@
 VIS_DEV = 16
 ROWS = 32
 LANES = 128
-GROUP = 8
+GROUP = 16
+DEPTH = 160
+FILTER_ROWS = 80
+FILTER_BAND = 656
+FILTER_DEPTH = 112
 SLOT_ROWS = 10
 
 gauss_widths = (1.0, 2.0, 4.0)
@@ -65,14 +69,14 @@
 
 def constants():
     values = filter_table(KR)
-    band = np.zeros((256, 48), np.float32)
+    band = np.zeros((2 * FILTER_BAND, FILTER_DEPTH), np.float32)
     for which, held in enumerate((SET_P, SET_Q)):
-        for y in range(16):
+        for y in range(FILTER_ROWS + 1):
             for row, b in enumerate(held):
-                band[which * 128 + y * 8 + row, y : y + TAPS] = values[:, b]
+                band[which * FILTER_BAND + y * 8 + row, y : y + TAPS] = values[:, b]
     columns = []
     for held in (COLS_P, COLS_Q):
-        wide = np.zeros((256, len(held) * LANES), np.float32)
+        wide = np.zeros((DEPTH, len(held) * LANES), np.float32)
         for place, a in enumerate(held):
             for j in range(LANES):
                 wide[j : j + TAPS, place * LANES + j] = values[:, a]
@@ -114,49 +118,64 @@
         ).astype(jnp.bfloat16)
 
 
-def fit_kernel(arrived, template, band, wide_p, wide_q, images, gram, details_out,
-               rows_p, rows_q, data, left_p, left_q, right_p, right_q, design,
+def fit_kernel(place, arrived, own, next_1, next_2, next_3, band, wide_p, wide_q,
+               images, gram, details_out,
+               template, rows, data, left_p, left_q, right_p, right_q, design,
                total, details, sem):
     data[...] = arrived[...].astype(jnp.float32)
     for c in range(2):
-        fields = data[pl.ds(8 + c, LANES, stride=SLOT_ROWS), :].T
-        details_out[c] = fields[0:8, :].astype(jnp.int32)
+        fields = data[pl.ds(8 + c, LANES, stride=SLOT_ROWS), :].T[0:8, :].astype(jnp.int32)
+        line = iota((8, LANES), 0)
+        at = (fields[1:2, :] * 9 + fields[2:3, :]) * 2
+        turn = (LANES - fields[3:4, :]) & 127
+        fields = jnp.where(line == 1, at, jnp.where(line == 2, turn, fields))
+        details_out[c] = fields
     copy = pltpu.make_async_copy(details_out, details, sem)
     copy.start()
-    for y in range(0, 240, 16):
-        depth = min(48, 256 - y)
-        made = jnp.dot(band[:, 0:depth], template[y : y + depth, :],
+    for m, part in enumerate((own, next_1, next_2, next_3)):
+        at = pl.multiple_of((place[0] ^ m) * 64, 64)
+        template[pl.ds(at, 64), :] = part[...]
+    for y0 in range(0, 240, FILTER_ROWS):
+        depth = min(FILTER_DEPTH, 256 - y0)
+        made = jnp.dot(band[:, 0:depth], template[y0 : y0 + depth, :],
                        preferred_element_type=jnp.float32)
-        made = made.astype(jnp.bfloat16).astype(jnp.float32)
-        rows_p[y * 8 : y * 8 + 128, :] = made[0:128]
-        rows_q[y * 8 : y * 8 + 128, :] = made[128:256]
+        for which in range(2):
+            for y in range(FILTER_ROWS):
+                if y0 + y < 236:
+                    first = which * FILTER_BAND + y * 8
+                    pair = made[first : first + 16, :].astype(jnp.bfloat16)
+                    for tile in range(8):
+                        rows[((y0 + y) * 9 + tile) * 2 + which] = pair[:, tile * LANES : (tile + 1) * LANES]
+    empty = jnp.zeros((16, LANES), jnp.bfloat16)
+    for y in range(236):
+        for which in range(2):
+            rows[(y * 9 + 8) * 2 + which] = empty
     total[...] = jnp.zeros_like(total)
     copy.wait()
     lane = iota((16, LANES), 1)
     sub = iota((8, LANES), 0)
     quarter = iota((ROWS, LANES), 1) >> 5
-
-    def step(g, carry):
+    groups = 2 * LANES // GROUP
+
+    def gather(g, side):
         for t in range(GROUP):
             c = t % 2
             src = g * (GROUP // 2) + t // 2
-            r = details[c, 1, src]
-            q = details[c, 2, src]
-            s = details[c, 3, src]
-            back = (LANES - s) & 127
-            keep = lane < LANES - s
-            for rows, left in ((rows_p, left_p), (rows_q, left_q)):
-                turned = []
-                for m in range(3):
-                    at = pl.multiple_of(jnp.minimum(q + m, 7) * LANES, LANES)
-                    piece = rows[pl.ds(pl.multiple_of(r * 8, 8), 16), pl.ds(at, LANES)]
-                    turned.append(pltpu.roll(piece, back, 1))
+            at = details[c, 1, src]
+            back = details[c, 2, src]
+            keep = lane < LANES - details[c, 3, src]
+            for which, left in enumerate((left_p, left_q)):
+                turned = [pltpu.roll(rows[at + 2 * m + which], back, 1) for m in range(3)]
                 for m in range(2):
-                    left[t * 16 : t * 16 + 16, m * LANES : (m + 1) * LANES] = jnp.where(
+                    left[side, t * 16 : t * 16 + 16, m * LANES : (m + 1) * LANES] = jnp.where(
                         keep, turned[m], turned[m + 1]
-                    ).astype(jnp.bfloat16)
-        right_p[...] = jnp.dot(left_p[...], wide_p[...], preferred_element_type=jnp.float32)
-        right_q[...] = jnp.dot(left_q[...], wide_q[...], preferred_element_type=jnp.float32)
+                    )
+
+    def filter_columns(side):
+        right_p[side] = jnp.dot(left_p[side, :, 0:DEPTH], wide_p[...], preferred_element_type=jnp.float32)
+        right_q[side] = jnp.dot(left_q[side, :, 0:DEPTH], wide_q[...], preferred_element_type=jnp.float32)
+
+    def combine(g, side):
         for t in range(GROUP):
             c = t % 2
             src = g * (GROUP // 2) + t // 2
@@ -165,11 +184,11 @@
 
                 def p(a):
                     k = COLS_P.index(a)
-                    return right_p[at : at + 8, k * LANES : (k + 1) * LANES]
+                    return right_p[side, at : at + 8, k * LANES : (k + 1) * LANES]
 
                 def q(a):
                     k = COLS_Q.index(a)
-                    return right_q[at : at + 8, k * LANES : (k + 1) * LANES]
+                    return right_q[side, at : at + 8, k * LANES : (k + 1) * LANES]
 
                 v0 = jnp.where(sub < 5, p(0), p(5))
                 v1 = jnp.where(sub < 4, p(1), jnp.where(sub == 7, 0.0, p(6)))
@@ -184,18 +203,31 @@
                 science = data[pl.ds(src * SLOT_ROWS + 2 * c + i, 1), :]
                 d1 = jnp.where(sub == 7, science, v1 * weight)
                 whole = jnp.concatenate([v0 * weight, d1, v2 * weight, v3 * weight], axis=0)
-                design[t * ROWS : (t + 1) * ROWS, lanes] = whole.astype(jnp.bfloat16)
+                design[side, t * ROWS : (t + 1) * ROWS, lanes] = whole.astype(jnp.bfloat16)
+
+    def accumulate(g, side, valid):
         for h in range(GROUP // 4):
-            part = design[h * 128 : (h + 1) * 128, :]
+            part = design[side, h * 128 : (h + 1) * 128, :]
             product = lax.dot_general(part, part, (((1,), (1,)), ((), ())),
                                       preferred_element_type=jnp.float32)
             for n in range(4):
                 t = h * 4 + n
                 v = details[t % 2, 0, g * (GROUP // 2) + t // 2]
-                total[v] += jnp.where(quarter == n, product[n * ROWS : (n + 1) * ROWS, :], 0.0)
+                mine = quarter == jnp.where(valid, n, -1)
+                total[v] += jnp.where(mine, product[n * ROWS : (n + 1) * ROWS, :], 0.0)
+
+    def step(j, carry):
+        for side in range(2):
+            g = 2 * j + side
+            old = g - 2
+            accumulate(jnp.clip(old, 0, groups - 1), side, (old >= 0) & (old < groups))
+            combine(jnp.clip(g - 1, 0, groups - 1), 1 - side)
+            filter_columns(side)
+            gather(jnp.minimum(g + 1, groups - 1), 1 - side)
         return carry
 
-    lax.fori_loop(0, 2 * LANES // GROUP, step, 0)
+    gather(0, 0)
+    lax.fori_loop(0, (groups + 2) // 2, step, 0)
     lane8 = iota((8, LANES), 1) >> 5
     for v in range(VIS_DEV):
         whole = total[v]
@@ -249,28 +281,41 @@
 
 
 def model_kernel(details, answers, images, model, wide, sums):
-    block = images.shape[0] // ROWS
-    g = pl.program_id(0)
-
-    @pl.when(g == 0)
-    def _():
-        turned = jnp.concatenate([answers[...], jnp.zeros((LANES - 8, LANES), jnp.float32)], axis=0).T
-        for v in range(VIS_DEV):
-            piece = turned[(v % 2) * ROWS : (v % 2) * ROWS + ROWS, v // 2 : v // 2 + 1]
-            wide[v] = jnp.broadcast_to(piece, (ROWS, LANES))
-
-    for t in range(block):
-        v = details[t % 2, 0, g * (block // 2) + t // 2]
-        for i in range(2):
-            lanes = slice(i * LANES, (i + 1) * LANES)
-            acc = wide[v, 0:8] * images[t * ROWS : t * ROWS + 8, lanes]
-            for m in range(1, 4):
-                acc = acc + wide[v, 8 * m : 8 * m + 8] * images[t * ROWS + 8 * m : t * ROWS + 8 * m + 8, lanes]
-            sums[(2 * t + i) * 8 : (2 * t + i) * 8 + 8, :] = acc
-    out = sums[pl.ds(0, 2 * block, stride=8), :]
-    for n in range(1, 8):
-        out = out + sums[pl.ds(n, 2 * block, stride=8), :]
-    model[...] = out.astype(jnp.bfloat16)
+    turned = jnp.concatenate([answers[...], jnp.zeros((LANES - 8, LANES), jnp.float32)], axis=0).T
+    for v in range(VIS_DEV):
+        piece = turned[(v % 2) * ROWS : (v % 2) * ROWS + ROWS, v // 2 : v // 2 + 1]
+        wide[v] = jnp.broadcast_to(piece, (ROWS, LANES))
+    block = 16
+
+    def step(g, carry):
+        for t in range(block):
+            v = details[t % 2, 0, g * (block // 2) + t // 2]
+            scale = [wide[v, 8 * m : 8 * m + 8] for m in range(4)]
+            first = pl.multiple_of((g * block + t) * ROWS, ROWS)
+            for i in range(2):
+                lanes = slice(i * LANES, (i + 1) * LANES)
+                acc = scale[0] * images[pl.ds(first, 8), lanes]
+                for m in range(1, 4):
+                    acc = acc + scale[m] * images[pl.ds(first + 8 * m, 8), lanes]
+                sums[(2 * t + i) * 8 : (2 * t + i) * 8 + 8, :] = acc
+        out = sums[pl.ds(0, 2 * block, stride=8), :]
+        for n in range(1, 8):
+            out = out + sums[pl.ds(n, 2 * block, stride=8), :]
+        model[pl.ds(pl.multiple_of(g * 2 * block, 2 * block), 2 * block), :] = out.astype(jnp.bfloat16)
+        return carry
+
+    lax.fori_loop(0, 2 * LANES // block, step, 0)
+
+
+def order_kernel(answers, out):
+    row, place = iota((LANES, NB), 0), iota((LANES, NB), 1)
+    for h in range(2):
+        chosen = row < 0
+        for k, at in enumerate(basis_rows()):
+            chosen = chosen | ((place == k) & (row == 32 * h + at))
+        out[pl.ds(h, 8, stride=2), :] = jnp.dot(
+            answers[...], jnp.where(chosen, 1.0, 0.0), precision=lax.Precision.HIGHEST,
+            preferred_element_type=jnp.float32)
 
 
 def final_kernel(slots, science, returned, out):
@@ -291,8 +336,8 @@
     return jax.ShapeDtypeStruct(dims, dtype)
 
 
-def params(**more):
-    return pltpu.CompilerParams(vmem_limit_bytes=60 << 20, **more)
+def params(mebibytes):
+    return pltpu.CompilerParams(vmem_limit_bytes=mebibytes << 20)
 
 
 def pack(science, sigma, dest, visit, offsets):
@@ -301,59 +346,61 @@
         out_shape=(shape((LANES * SLOT_ROWS, LANES), jnp.bfloat16), shape((8, LANES), jnp.int32)),
         in_specs=vmem(5), out_specs=tuple(vmem(2)),
         scratch_shapes=[pltpu.VMEM((5 * LANES, LANES), jnp.bfloat16)],
-        compiler_params=params(), name="pack",
+        compiler_params=params(8), name="pack",
     )(science, sigma, dest, visit, offsets)
 
 
-def fit(arrived, template, band, wide_p, wide_q):
+def fit(place, arrived, parts, band, wide_p, wide_q):
     return pl.pallas_call(
         fit_kernel,
         out_shape=(shape((2 * LANES * ROWS, 2 * LANES)), shape((VIS_DEV * 8, LANES)),
                    shape((2, 8, LANES), jnp.int32)),
-        in_specs=vmem(5), out_specs=tuple(vmem(3)),
+        in_specs=[pl.BlockSpec(memory_space=pltpu.SMEM)] + vmem(8), out_specs=tuple(vmem(3)),
         scratch_shapes=[
-            pltpu.VMEM((1920, 1024), jnp.float32), pltpu.VMEM((1920, 1024), jnp.float32),
+            pltpu.VMEM((256, 1024), jnp.bfloat16),
+            pltpu.VMEM((236 * 9 * 2, 16, LANES), jnp.bfloat16),
             pltpu.VMEM((LANES * SLOT_ROWS, LANES), jnp.float32),
-            pltpu.VMEM((GROUP * 16, 256), jnp.bfloat16), pltpu.VMEM((GROUP * 16, 256), jnp.bfloat16),
-            pltpu.VMEM((GROUP * 16, len(COLS_P) * LANES), jnp.float32),
-            pltpu.VMEM((GROUP * 16, len(COLS_Q) * LANES), jnp.float32),
-            pltpu.VMEM((GROUP * ROWS, 256), jnp.bfloat16),
+            pltpu.VMEM((2, GROUP * 16, 256), jnp.bfloat16), pltpu.VMEM((2, GROUP * 16, 256), jnp.bfloat16),
+            pltpu.VMEM((2, GROUP * 16, len(COLS_P) * LANES), jnp.float32),
+            pltpu.VMEM((2, GROUP * 16, len(COLS_Q) * LANES), jnp.float32),
+            pltpu.VMEM((2, GROUP * ROWS, 256), jnp.bfloat16),
             pltpu.VMEM((VIS_DEV, ROWS, LANES), jnp.float32),
             pltpu.SMEM((2, 8, LANES), jnp.int32), pltpu.SemaphoreType.DMA,
         ],
-        compiler_params=params(), name="fit",
-    )(arrived, template, band, wide_p, wide_q)
+        compiler_params=params(40), name="fit",
+    )(place, arrived, *parts, band, wide_p, wide_q)
 
 
 def middle(parts):
     return pl.pallas_call(middle_kernel, out_shape=shape((16,) + parts.shape[1:]),
-                          in_specs=vmem(1), out_specs=vmem(1)[0], name="middle")(parts)
+                          in_specs=vmem(1), out_specs=vmem(1)[0], compiler_params=params(4), name="middle")(parts)
 
 
 def solve(parts):
     return pl.pallas_call(solve_kernel, out_shape=shape((8, 1, LANES)),
-                          in_specs=vmem(1), out_specs=vmem(1)[0], name="solve")(parts)
+                          in_specs=vmem(1), out_specs=vmem(1)[0], compiler_params=params(4), name="solve")(parts)
 
 
 def model_of(details, answers, images):
-    block = 32
     return pl.pallas_call(
         model_kernel,
         out_shape=shape((4 * LANES, LANES), jnp.bfloat16),
-        grid=(2 * LANES // block,),
-        in_specs=[pl.BlockSpec(memory_space=pltpu.SMEM),
-                  pl.BlockSpec((8, LANES), lambda g: (0, 0)),
-                  pl.BlockSpec((block * ROWS, 2 * LANES), lambda g: (g, 0))],
-        out_specs=pl.BlockSpec((2 * block, LANES), lambda g: (g, 0)),
+        in_specs=[pl.BlockSpec(memory_space=pltpu.SMEM)] + vmem(2),
+        out_specs=vmem(1)[0],
         scratch_shapes=[pltpu.VMEM((VIS_DEV, ROWS, LANES), jnp.float32),
-                        pltpu.VMEM((block * 16, LANES), jnp.float32)],
-        compiler_params=params(), name="model",
+                        pltpu.VMEM((16 * 16, LANES), jnp.float32)],
+        compiler_params=params(14), name="model",
     )(details, answers, images)
+
+
+def order(answers):
+    return pl.pallas_call(order_kernel, out_shape=shape((VIS_DEV, NB)), in_specs=vmem(1),
+                          out_specs=vmem(1)[0], compiler_params=params(4), name="order")(answers)
 
 
 def final(slots, science, returned):
     return pl.pallas_call(final_kernel, out_shape=shape((2 * LANES, LANES)),
-                          in_specs=vmem(3), out_specs=vmem(1)[0], name="final")(slots, science, returned)
+                          in_specs=vmem(3), out_specs=vmem(1)[0], compiler_params=params(4), name="final")(slots, science, returned)
 
 
 def exchange(values, groups=None):
@@ -366,20 +413,21 @@
     planes = [[z * 8 + i for i in range(8)] for z in range(patches // 8)]
     lines = [[z * 8 + i for z in range(patches // 8)] for i in range(8)]
     band, wide_p, wide_q = constants()
-    whole_template = lax.all_gather(template[0].astype(jnp.bfloat16), "visit", axis=0, tiled=True)
+    own = template[0].astype(jnp.bfloat16)
+    parts = [own] + [lax.ppermute(own, "visit", [(x, x ^ m) for x in range(4)]) for m in (1, 2, 3)]
+    place = lax.axis_index("visit").astype(jnp.int32).reshape(1)
     science_rows = science.reshape(2 * LANES, LANES)
     packed, slots = pack(science_rows, inverse_sigma.reshape(2 * LANES, LANES),
                          destination.reshape(1, LANES), visit_local.reshape(1, LANES), offsets.T)
     arrived = exchange(packed.reshape(patches, 5, 2, LANES)).reshape(LANES * SLOT_ROWS, LANES)
-    images, gram, details = fit(arrived, whole_template, band, wide_p, wide_q)
+    images, gram, details = fit(place, arrived, parts, band, wide_p, wide_q)
     parts = exchange(gram.reshape(8, 16, LANES), planes)
     parts = exchange(middle(parts), lines)
     answers = exchange(solve(parts), planes).reshape(8, LANES)
     model = model_of(details, answers, images)
     returned = exchange(model.reshape(patches, 2, 2, LANES)).reshape(4 * LANES, LANES)
     difference = final(slots, science_rows, returned)
-    table = jnp.concatenate([answers[:, 0:32], answers[:, 32:64]], axis=1).reshape(VIS_DEV, ROWS)
-    coefficients = jnp.stack([table[:, k] for k in basis_rows()], axis=1)
+    coefficients = order(answers)
     return difference.reshape(science.shape), coefficients
 
 

time: 152 us -> 130 us (0.86)
  Pallas kernels: 43.5 us -> 20.9 us
  blocking collectives: 51.1 us -> 36.4 us
  starting transfers between devices: 26.9 us -> 35.9 us
  local copies, waits for them, and re-layouts: 2.98 us -> 6.64 us
  waiting for transfers between devices: 24.6 us -> 27.9 us
    pallas_call x1, Pallas kernels: 26.6 us -> 11.9 us  [fit(): pl.pallas_call(fit_kernel, out_shape=(shape((2 * LANES * ROWS, 2 * LANES)...]
    all_gather x1 -> x0, blocking collectives: 12.1 us -> none  [per_device(): lax.all_gather(template[0].astype(jnp.bfloat16), 'visit', axis=0, tiled=T...]
    ppermute x0 -> x3, starting transfers between devices: none -> 8.98 us  [per_device(): lax.ppermute(own, 'visit', [(x, x ^ m) for x in range(4)])]
    unnamed x6 -> x18, local copies, waits for them, and re-layouts: 1.92 us -> 6.64 us
    ppermute x0 -> x3, waiting for transfers between devices: none -> 3.83 us  [per_device(): lax.ppermute(own, 'visit', [(x, x ^ m) for x in range(4)])]
    pallas_call x1, Pallas kernels: 7.09 us -> 3.31 us  [model_of(): pl.pallas_call(model_kernel, out_shape=shape((4 * LANES, LANES), jnp.bflo...]
    all_to_all x3, blocking collectives: 39 us -> 36.4 us  [exchange(): lax.all_to_all(values, 'patch', split_axis=0, concat_axis=0, tiled=True,...]
  transfers between devices with their start and end apart: 2 -> 5, of which waited for: 2 -> 4; matrix products, arithmetic and copies ran while one was open for 1% -> 1% of each run, Pallas kernels for 0% -> 1%
where the time goes in v2:
time: 130 us; the launch traced here: 129 us
  blocking collectives  36.4 us (28%)
  starting transfers between devices  35.9 us (28%)
  waiting for transfers between devices  27.9 us (21%)
  Pallas kernels  20.9 us (16%)
  local copies, waits for them, and re-layouts  6.64 us (5%)
    all_to_all x3, blocking collectives, exchange(): lax.all_to_all(values, 'patch', split_axis=0, concat_axis=0, tiled=True,...  36.4 us
    all_to_all x2, starting transfers between devices, exchange(): lax.all_to_all(values, 'patch', split_axis=0, concat_axis=0, tiled=True,...  26.9 us
    all_to_all x2, waiting for transfers between devices, exchange(): lax.all_to_all(values, 'patch', split_axis=0, concat_axis=0, tiled=True,...  24.1 us
    pallas_call x1, Pallas kernels, fit(): pl.pallas_call(fit_kernel, out_shape=(shape((2 * LANES * ROWS, 2 * LANES)...  11.9 us
    ppermute x3, starting transfers between devices, per_device(): lax.ppermute(own, 'visit', [(x, x ^ m) for x in range(4)])  8.98 us
    unnamed x18, local copies, waits for them, and re-layouts  6.64 us
    ppermute x3, waiting for transfers between devices, per_device(): lax.ppermute(own, 'visit', [(x, x ^ m) for x in range(4)])  3.83 us
    pallas_call x1, Pallas kernels, model_of(): pl.pallas_call(model_kernel, out_shape=shape((4 * LANES, LANES), jnp.bflo...  3.31 us
  transfers between devices with their start and end apart: 5, of which 4 were waited for; matrix products, arithmetic and copies ran while one was open for 1% of the time, Pallas kernels for 1%

profile of v2, /device:TPU:1, one launch (start us, length us, event | category | flops | bytes accessed | tf_op | source)
XLA Modules:
  0.0 129.4 jit_solution(9297684393682608372)
XLA Ops:
  0.6 0.0 copy-start
  0.6 0.9 copy-done
  1.5 0.0 copy-start.5
  1.5 0.9 copy-done.5
  2.4 0.0 copy-start.6
  2.4 0.7 copy-done.6
  3.1 0.0 copy-start.7
  3.1 0.7 copy-done.7
  3.8 0.0 copy-start.8
  3.8 0.7 copy-done.8
  4.4 0.0 copy-start.1
  4.4 1.5 %pack.1 = (bf16[1280,128]{1,0:T(8,128)(2,1)}, s32[8,128]{1,0:T(8,128)S(1)}) custom-call(f32[256,128]{1,0:T(8,128)S(1)} %bitcast.16, f32[256,128]{1,0:T(8,128)S(1)} %bitcast.19, s32[1,128]{1,0:T(1,128)S(1)} %bitcast.24, s32[1,128]{1,0:T(1,128)S(1)} %bitcast.25, s32[2,128]{1,0:T(2,128)S(1)} %bitcast.23), custom_call_target="tpu_custom_call" | custom-call | tf_op jit(solution)/shard_map/pack/pallas_call | solution.py:344
  5.9 20.5 %all-to-all-start = ((bf16[128,5,2,128]{3,2,1,0:T(2,128)(2,1)}), bf16[128,5,2,128]{3,2,1,0:T(2,128)(2,1)S(1)}, u32[]{:S(2)}, u32[]{:S(2)}) async-start(bf16[128,5,2,128]{3,2,1,0:T(2,128)(2,1)} %bitcast.6), calls=%async_computation | async-start | bytes 655360 | tf_op jit(solution)/shard_map/all_to_all | solution.py:407
  26.5 1.0 convert_bitcast_fusion.own
  27.4 4.4 %collective-permute-start.2 = (bf16[64,1024]{1,0:T(8,128)(2,1)S(1)}, bf16[64,1024]{1,0:T(8,128)(2,1)S(1)}, u32[]{:S(2)}, u32[]{:S(2)}) collective-permute-start(bf16[64,1024]{1,0:T(8,128)(2,1)S(1)} %convert_bitcast_fusion.own), channel_id=1, source_target_pairs={{0,3},{1,2},{2,1},{3,0},{4,7},{5,6},{6,5},{7,4},{8,11},{9,10},{10,... | collective-permute-start | bytes 393224 | tf_op jit(solution)/shard_map/ppermute | solution.py:417
  31.8 2.4 %collective-permute-start.1 = (bf16[64,1024]{1,0:T(8,128)(2,1)S(1)}, bf16[64,1024]{1,0:T(8,128)(2,1)S(1)}, u32[]{:S(2)}, u32[]{:S(2)}) collective-permute-start(bf16[64,1024]{1,0:T(8,128)(2,1)S(1)} %convert_bitcast_fusion.own), channel_id=1, source_target_pairs={{0,2},{1,3},{2,0},{3,1},{4,6},{5,7},{6,4},{7,5},{8,10},{9,11},{10,... | collective-permute-start | bytes 393224 | tf_op jit(solution)/shard_map/ppermute | solution.py:417
  34.3 2.2 %collective-permute-start = (bf16[64,1024]{1,0:T(8,128)(2,1)S(1)}, bf16[64,1024]{1,0:T(8,128)(2,1)S(1)}, u32[]{:S(2)}, u32[]{:S(2)}) collective-permute-start(bf16[64,1024]{1,0:T(8,128)(2,1)S(1)} %convert_bitcast_fusion.own), channel_id=1, source_target_pairs={{0,1},{1,0},{2,3},{3,2},{4,5},{5,4},{6,7},{7,6},{8,9},{9,8},{10,11... | collective-permute-start | bytes 393224 | tf_op jit(solution)/shard_map/ppermute | solution.py:417
  36.4 0.0 collective-permute-done.2.next_3
  36.4 2.9 %collective-permute-done.1.next_2 = bf16[64,1024]{1,0:T(8,128)(2,1)S(1)} collective-permute-done((bf16[64,1024]{1,0:T(8,128)(2,1)S(1)}, bf16[64,1024]{1,0:T(8,128)(2,1)S(1)}, u32[]{:S(2)}, u32[]{:S(2)}) %collective-permute-start.1) | collective-permute-done | bytes 131104 | tf_op jit(solution)/shard_map/ppermute | solution.py:417
  39.3 0.9 collective-permute-done.next_1
  40.3 8.9 %all-to-all-done = bf16[128,5,2,128]{3,2,1,0:T(2,128)(2,1)S(1)} async-done(((bf16[128,5,2,128]{3,2,1,0:T(2,128)(2,1)}), bf16[128,5,2,128]{3,2,1,0:T(2,128)(2,1)S(1)}, u32[]{:S(2)}, u32[]{:S(2)}) %all-to-all-start) | async-done | bytes 327712 | tf_op jit(solution)/shard_map/all_to_all | solution.py:407
  49.2 0.0 copy-start.2
  49.2 1.0 copy-done.2
  50.1 0.0 copy-start.3
  50.1 0.9 copy-done.3
  51.1 0.0 copy-start.4
  51.1 0.9 copy-done.4
  52.0 11.9 %fit.1 = (f32[8192,256]{1,0:T(8,128)S(1)}, f32[128,128]{1,0:T(8,128)S(1)}, s32[2,8,128]{2,1,0:T(8,128)S(1)}) custom-call(s32[1]{0:T(128)} %bitcast.5.place, bf16[1280,128]{1,0:T(8,128)(2,1)S(1)} %bitcast.15, bf16[64,1024]{1,0:T(8,128)(2,1)S(1)} %convert_bitcast_fusion.own, bf16[64,1024]{1,0:T(8,128)(2,1)S(1)} %collective-permute-done.next_1, ...), custom_call_target="tpu_custom_call" | custom-call | tf_op jit(solution)/shard_map/fit/pallas_call | solution.py:354
  63.9 11.2 %all_to_all.25.parts = f32[8,16,128]{2,1,0:T(8,128)S(1)} all-to-all(f32[8,16,128]{2,1,0:T(8,128)S(1)} %bitcast.20), channel_id=1, replica_groups={{0,4,8,12,16,20,24,28},{32,36,40,44,48,52,56,60},{64,68,72,76,80,84,88,..., dimensions={0} | all-to-all | bytes 131072 | tf_op jit(solution)/shard_map/all_to_all | solution.py:407
  75.2 14.5 %all_to_all.26.parts = f32[16,16,128]{2,1,0:T(8,128)S(1)} all-to-all(f32[16,16,128]{2,1,0:T(8,128)S(1)} %middle.1), channel_id=1, replica_groups={{0,32,64,96,128,160,192,224,256,288,320,352,384,416,448,480},{4,36,68,1..., dimensions={0} | all-to-all | bytes 262144 | tf_op jit(solution)/shard_map/all_to_all | solution.py:407
  89.7 2.5 %solve.1 = f32[8,1,128]{2,1,0:T(1,128)S(1)} custom-call(f32[16,16,128]{2,1,0:T(8,128)S(1)} %all_to_all.26.parts), custom_call_target="tpu_custom_call" | custom-call | tf_op jit(solution)/shard_map/solve/pallas_call | solution.py:380
  92.1 10.6 %all_to_all.27 = f32[8,1,128]{2,1,0:T(1,128)S(1)} all-to-all(f32[8,1,128]{2,1,0:T(1,128)S(1)} %solve.1), channel_id=1, replica_groups={{0,4,8,12,16,20,24,28},{32,36,40,44,48,52,56,60},{64,68,72,76,80,84,88,..., dimensions={0} | all-to-all | bytes 8192 | tf_op jit(solution)/shard_map/all_to_all | solution.py:407
  102.8 3.3 %model.1 = bf16[512,128]{1,0:T(8,128)(2,1)} custom-call(s32[2,8,128]{2,1,0:T(8,128)S(1)} %get-tuple-element.9.details, f32[8,128]{1,0:T(8,128)S(1)} %bitcast.21, f32[8192,256]{1,0:T(8,128)S(1)} %get-tuple-element.11.images), custom_call_target="tpu_custom_call" | custom-call | tf_op jit(solution)/shard_map/model/pallas_call | solution.py:385
  106.1 6.4 %all-to-all-start.4 = ((bf16[128,2,2,128]{3,2,1,0:T(2,128)(2,1)}), bf16[128,2,2,128]{3,2,1,0:T(2,128)(2,1)S(1)}, u32[]{:S(2)}, u32[]{:S(2)}) async-start(bf16[128,2,2,128]{3,2,1,0:T(2,128)(2,1)} %bitcast.11), calls=%async_computation.4 | async-start | bytes 262144 | tf_op jit(solution)/shard_map/all_to_all | solution.py:407
  112.5 0.8 order.1
  113.3 15.2 %all-to-all-done.4 = bf16[128,2,2,128]{3,2,1,0:T(2,128)(2,1)S(1)} async-done(((bf16[128,2,2,128]{3,2,1,0:T(2,128)(2,1)}), bf16[128,2,2,128]{3,2,1,0:T(2,128)(2,1)S(1)}, u32[]{:S(2)}, u32[]{:S(2)}) %all-to-all-start.4) | async-done | bytes 131104 | tf_op jit(solution)/shard_map/all_to_all | solution.py:407
  128.5 0.0 copy-done.1
  128.5 0.9 final.1
  (1 shorter events, 0.0 us)
Async XLA Ops:
  0.6 0.9 copy-start
  1.5 0.9 copy-start.5
  2.4 0.7 copy-start.6
  3.1 0.7 copy-start.7
  3.8 0.7 copy-start.8
  4.4 124.0 %copy-start.1 = (f32[128,2,128]{2,1,0:T(2,128)S(1)}, f32[128,2,128]{2,1,0:T(2,128)}, u32[]{:S(2)}) copy-start(f32[128,2,128]{2,1,0:T(2,128)} %param.9) | copy-start | bytes 393220
  5.9 43.3 %all-to-all-start = ((bf16[128,5,2,128]{3,2,1,0:T(2,128)(2,1)}), bf16[128,5,2,128]{3,2,1,0:T(2,128)(2,1)S(1)}, u32[]{:S(2)}, u32[]{:S(2)}) async-start(bf16[128,5,2,128]{3,2,1,0:T(2,128)(2,1)} %bitcast.6), calls=%async_computation | async-start | bytes 655360 | tf_op jit(solution)/shard_map/all_to_all | solution.py:407
  27.4 9.0 %collective-permute-start.2 = (bf16[64,1024]{1,0:T(8,128)(2,1)S(1)}, bf16[64,1024]{1,0:T(8,128)(2,1)S(1)}, u32[]{:S(2)}, u32[]{:S(2)}) collective-permute-start(bf16[64,1024]{1,0:T(8,128)(2,1)S(1)} %convert_bitcast_fusion.own), channel_id=1, source_target_pairs={{0,3},{1,2},{2,1},{3,0},{4,7},{5,6},{6,5},{7,4},{8,11},{9,10},{10,... | collective-permute-start | bytes 393224 | tf_op jit(solution)/shard_map/ppermute | solution.py:417
  31.8 7.5 %collective-permute-start.1 = (bf16[64,1024]{1,0:T(8,128)(2,1)S(1)}, bf16[64,1024]{1,0:T(8,128)(2,1)S(1)}, u32[]{:S(2)}, u32[]{:S(2)}) collective-permute-start(bf16[64,1024]{1,0:T(8,128)(2,1)S(1)} %convert_bitcast_fusion.own), channel_id=1, source_target_pairs={{0,2},{1,3},{2,0},{3,1},{4,6},{5,7},{6,4},{7,5},{8,10},{9,11},{10,... | collective-permute-start | bytes 393224 | tf_op jit(solution)/shard_map/ppermute | solution.py:417
  34.3 6.0 %collective-permute-start = (bf16[64,1024]{1,0:T(8,128)(2,1)S(1)}, bf16[64,1024]{1,0:T(8,128)(2,1)S(1)}, u32[]{:S(2)}, u32[]{:S(2)}) collective-permute-start(bf16[64,1024]{1,0:T(8,128)(2,1)S(1)} %convert_bitcast_fusion.own), channel_id=1, source_target_pairs={{0,1},{1,0},{2,3},{3,2},{4,5},{5,4},{6,7},{7,6},{8,9},{9,8},{10,11... | collective-permute-start | bytes 393224 | tf_op jit(solution)/shard_map/ppermute | solution.py:417
  49.2 1.0 copy-start.2
  50.1 0.9 copy-start.3
  51.1 0.9 copy-start.4
  106.1 22.4 %all-to-all-start.4 = ((bf16[128,2,2,128]{3,2,1,0:T(2,128)(2,1)}), bf16[128,2,2,128]{3,2,1,0:T(2,128)(2,1)S(1)}, u32[]{:S(2)}, u32[]{:S(2)}) async-start(bf16[128,2,2,128]{3,2,1,0:T(2,128)(2,1)} %bitcast.11), calls=%async_computation.4 | async-start | bytes 262144 | tf_op jit(solution)/shard_map/all_to_all | solution.py:407

commit v3 on v2

--- a/solution.py
+++ b/solution.py
@@ -118,9 +118,18 @@
         ).astype(jnp.bfloat16)
 
 
-def fit_kernel(place, arrived, own, next_1, next_2, next_3, band, wide_p, wide_q,
-               images, gram, details_out,
-               template, rows, data, left_p, left_q, right_p, right_q, design,
+def keep_kernel(place, own, next_1, next_2, next_3, band, wide_p, wide_q,
+                template, kept_band, kept_p, kept_q):
+    for m, part in enumerate((own, next_1, next_2, next_3)):
+        at = pl.multiple_of((place[0] ^ m) * 64, 64)
+        template[pl.ds(at, 64), :] = part[...]
+    kept_band[...] = band[...]
+    kept_p[...] = wide_p[...]
+    kept_q[...] = wide_q[...]
+
+
+def fit_kernel(arrived, template, band, wide_p, wide_q, images, gram, details_out,
+               rows, data, left_p, left_q, right_p, right_q, design,
                total, details, sem):
     data[...] = arrived[...].astype(jnp.float32)
     for c in range(2):
@@ -132,9 +141,6 @@
         details_out[c] = fields
     copy = pltpu.make_async_copy(details_out, details, sem)
     copy.start()
-    for m, part in enumerate((own, next_1, next_2, next_3)):
-        at = pl.multiple_of((place[0] ^ m) * 64, 64)
-        template[pl.ds(at, 64), :] = part[...]
     for y0 in range(0, 240, FILTER_ROWS):
         depth = min(FILTER_DEPTH, 256 - y0)
         made = jnp.dot(band[:, 0:depth], template[y0 : y0 + depth, :],
@@ -205,7 +211,7 @@
                 whole = jnp.concatenate([v0 * weight, d1, v2 * weight, v3 * weight], axis=0)
                 design[side, t * ROWS : (t + 1) * ROWS, lanes] = whole.astype(jnp.bfloat16)
 
-    def accumulate(g, side, valid):
+    def accumulate(g, side):
         for h in range(GROUP // 4):
             part = design[side, h * 128 : (h + 1) * 128, :]
             product = lax.dot_general(part, part, (((1,), (1,)), ((), ())),
@@ -213,21 +219,27 @@
             for n in range(4):
                 t = h * 4 + n
                 v = details[t % 2, 0, g * (GROUP // 2) + t // 2]
-                mine = quarter == jnp.where(valid, n, -1)
-                total[v] += jnp.where(mine, product[n * ROWS : (n + 1) * ROWS, :], 0.0)
+                total[v] += jnp.where(quarter == n, product[n * ROWS : (n + 1) * ROWS, :], 0.0)
 
     def step(j, carry):
         for side in range(2):
             g = 2 * j + side
-            old = g - 2
-            accumulate(jnp.clip(old, 0, groups - 1), side, (old >= 0) & (old < groups))
-            combine(jnp.clip(g - 1, 0, groups - 1), 1 - side)
+            accumulate(g - 2, side)
+            combine(g - 1, 1 - side)
             filter_columns(side)
             gather(jnp.minimum(g + 1, groups - 1), 1 - side)
         return carry
 
     gather(0, 0)
-    lax.fori_loop(0, (groups + 2) // 2, step, 0)
+    filter_columns(0)
+    gather(1, 1)
+    combine(0, 0)
+    filter_columns(1)
+    gather(2, 0)
+    lax.fori_loop(1, groups // 2, step, 0)
+    accumulate(groups - 2, 0)
+    combine(groups - 1, 1)
+    accumulate(groups - 1, 1)
     lane8 = iota((8, LANES), 1) >> 5
     for v in range(VIS_DEV):
         whole = total[v]
@@ -288,15 +300,16 @@
     block = 16
 
     def step(g, carry):
+        near = images.at[pl.ds(pl.multiple_of(g * block * ROWS, block * ROWS), block * ROWS), :]
         for t in range(block):
             v = details[t % 2, 0, g * (block // 2) + t // 2]
             scale = [wide[v, 8 * m : 8 * m + 8] for m in range(4)]
-            first = pl.multiple_of((g * block + t) * ROWS, ROWS)
+            first = t * ROWS
             for i in range(2):
                 lanes = slice(i * LANES, (i + 1) * LANES)
-                acc = scale[0] * images[pl.ds(first, 8), lanes]
+                acc = scale[0] * near[first : first + 8, lanes]
                 for m in range(1, 4):
-                    acc = acc + scale[m] * images[pl.ds(first + 8 * m, 8), lanes]
+                    acc = acc + scale[m] * near[first + 8 * m : first + 8 * m + 8, lanes]
                 sums[(2 * t + i) * 8 : (2 * t + i) * 8 + 8, :] = acc
         out = sums[pl.ds(0, 2 * block, stride=8), :]
         for n in range(1, 8):
@@ -346,18 +359,26 @@
         out_shape=(shape((LANES * SLOT_ROWS, LANES), jnp.bfloat16), shape((8, LANES), jnp.int32)),
         in_specs=vmem(5), out_specs=tuple(vmem(2)),
         scratch_shapes=[pltpu.VMEM((5 * LANES, LANES), jnp.bfloat16)],
-        compiler_params=params(8), name="pack",
+        compiler_params=params(60), name="pack",
     )(science, sigma, dest, visit, offsets)
 
 
-def fit(place, arrived, parts, band, wide_p, wide_q):
+def keep(place, parts, tables):
+    return pl.pallas_call(
+        keep_kernel,
+        out_shape=(shape((256, 1024), jnp.bfloat16),) + tuple(shape(t.shape, t.dtype) for t in tables),
+        in_specs=[pl.BlockSpec(memory_space=pltpu.SMEM)] + vmem(7), out_specs=tuple(vmem(4)),
+        compiler_params=params(8), name="keep",
+    )(place, *parts, *tables)
+
+
+def fit(arrived, template, band, wide_p, wide_q):
     return pl.pallas_call(
         fit_kernel,
         out_shape=(shape((2 * LANES * ROWS, 2 * LANES)), shape((VIS_DEV * 8, LANES)),
                    shape((2, 8, LANES), jnp.int32)),
-        in_specs=[pl.BlockSpec(memory_space=pltpu.SMEM)] + vmem(8), out_specs=tuple(vmem(3)),
+        in_specs=vmem(5), out_specs=tuple(vmem(3)),
         scratch_shapes=[
-            pltpu.VMEM((256, 1024), jnp.bfloat16),
             pltpu.VMEM((236 * 9 * 2, 16, LANES), jnp.bfloat16),
             pltpu.VMEM((LANES * SLOT_ROWS, LANES), jnp.float32),
             pltpu.VMEM((2, GROUP * 16, 256), jnp.bfloat16), pltpu.VMEM((2, GROUP * 16, 256), jnp.bfloat16),
@@ -368,7 +389,7 @@
             pltpu.SMEM((2, 8, LANES), jnp.int32), pltpu.SemaphoreType.DMA,
         ],
         compiler_params=params(40), name="fit",
-    )(place, arrived, *parts, band, wide_p, wide_q)
+    )(arrived, template, band, wide_p, wide_q)
 
 
 def middle(parts):
@@ -412,15 +433,15 @@
     patches = lax.axis_size("patch")
     planes = [[z * 8 + i for i in range(8)] for z in range(patches // 8)]
     lines = [[z * 8 + i for z in range(patches // 8)] for i in range(8)]
-    band, wide_p, wide_q = constants()
     own = template[0].astype(jnp.bfloat16)
     parts = [own] + [lax.ppermute(own, "visit", [(x, x ^ m) for x in range(4)]) for m in (1, 2, 3)]
     place = lax.axis_index("visit").astype(jnp.int32).reshape(1)
     science_rows = science.reshape(2 * LANES, LANES)
     packed, slots = pack(science_rows, inverse_sigma.reshape(2 * LANES, LANES),
                          destination.reshape(1, LANES), visit_local.reshape(1, LANES), offsets.T)
+    kept = keep(place, parts, constants())
     arrived = exchange(packed.reshape(patches, 5, 2, LANES)).reshape(LANES * SLOT_ROWS, LANES)
-    images, gram, details = fit(place, arrived, parts, band, wide_p, wide_q)
+    images, gram, details = fit(arrived, *kept)
     parts = exchange(gram.reshape(8, 16, LANES), planes)
     parts = exchange(middle(parts), lines)
     answers = exchange(solve(parts), planes).reshape(8, LANES)

time: 130 us -> 125 us (0.962)
  local copies, waits for them, and re-layouts: 6.64 us -> 2.86 us
  waiting for transfers between devices: 27.9 us -> 24.9 us
  blocking collectives: 36.4 us -> 39.1 us
    unnamed x18 -> x10, local copies, waits for them, and re-layouts: 6.64 us -> 2.86 us
    all_to_all x2, waiting for transfers between devices: 24.1 us -> 21.1 us  [exchange(): lax.all_to_all(values, 'patch', split_axis=0, concat_axis=0, tiled=True,...]
    all_to_all x3, blocking collectives: 36.4 us -> 39.1 us  [exchange(): lax.all_to_all(values, 'patch', split_axis=0, concat_axis=0, tiled=True,...]
where the time goes in v3:
time: 125 us
  blocking collectives  39.1 us (31%)
  starting transfers between devices  35.9 us (29%)
  waiting for transfers between devices  24.9 us (20%)
  Pallas kernels  20.1 us (16%)
  local copies, waits for them, and re-layouts  2.86 us (2%)
    all_to_all x3, blocking collectives, exchange(): lax.all_to_all(values, 'patch', split_axis=0, concat_axis=0, tiled=True,...  39.1 us
    all_to_all x2, starting transfers between devices, exchange(): lax.all_to_all(values, 'patch', split_axis=0, concat_axis=0, tiled=True,...  26.9 us
    all_to_all x2, waiting for transfers between devices, exchange(): lax.all_to_all(values, 'patch', split_axis=0, concat_axis=0, tiled=True,...  21.1 us
    pallas_call x1, Pallas kernels, fit(): pl.pallas_call(fit_kernel, out_shape=(shape((2 * LANES * ROWS, 2 * LANES)...  10.8 us
    ppermute x3, starting transfers between devices, per_device(): lax.ppermute(own, 'visit', [(x, x ^ m) for x in range(4)])  8.98 us
    ppermute x3, waiting for transfers between devices, per_device(): lax.ppermute(own, 'visit', [(x, x ^ m) for x in range(4)])  3.82 us
    unnamed x10, local copies, waits for them, and re-layouts  2.86 us
    pallas_call x1, Pallas kernels, model_of(): pl.pallas_call(model_kernel, out_shape=shape((4 * LANES, LANES), jnp.bflo...  2.5 us
  transfers between devices with their start and end apart: 5, of which 4 were waited for; matrix products, arithmetic and copies ran while one was open for 1% of the time, Pallas kernels for 1%

profile of v3, /device:TPU:1, one launch (start us, length us, event | category | flops | bytes accessed | tf_op | source)
XLA Modules:
  0.0 124.6 jit_solution(8390005742411093070)
XLA Ops:
  0.6 0.0 copy-start
  0.6 2.5 %pack.1 = (bf16[1280,128]{1,0:T(8,128)(2,1)}, s32[8,128]{1,0:T(8,128)}) custom-call(f32[256,128]{1,0:T(8,128)} %bitcast.16, f32[256,128]{1,0:T(8,128)} %bitcast.24, s32[1,128]{1,0:T(1,128)} %bitcast.26, s32[1,128]{1,0:T(1,128)} %bitcast.27, s32[2,128]{1,0:T(2,128)} %bitcast.25), custom_call_target="tpu_custom_call" | custom-call | tf_op jit(solution)/shard_map/pack/pallas_call | solution.py:357
  3.1 0.0 copy-start.4
  3.1 20.7 %all-to-all-start = ((bf16[128,5,2,128]{3,2,1,0:T(2,128)(2,1)}), bf16[128,5,2,128]{3,2,1,0:T(2,128)(2,1)S(1)}, u32[]{:S(2)}, u32[]{:S(2)}) async-start(bf16[128,5,2,128]{3,2,1,0:T(2,128)(2,1)} %bitcast.22), calls=%async_computation | async-start | bytes 655360 | tf_op jit(solution)/shard_map/all_to_all | solution.py:428
  23.8 1.0 convert_bitcast_fusion.own
  24.8 4.4 %collective-permute-start.2 = (bf16[64,1024]{1,0:T(8,128)(2,1)S(1)}, bf16[64,1024]{1,0:T(8,128)(2,1)S(1)}, u32[]{:S(2)}, u32[]{:S(2)}) collective-permute-start(bf16[64,1024]{1,0:T(8,128)(2,1)S(1)} %convert_bitcast_fusion.own), channel_id=1, source_target_pairs={{0,3},{1,2},{2,1},{3,0},{4,7},{5,6},{6,5},{7,4},{8,11},{9,10},{10,... | collective-permute-start | bytes 393224 | tf_op jit(solution)/shard_map/ppermute | solution.py:437
  29.2 2.4 %collective-permute-start.1 = (bf16[64,1024]{1,0:T(8,128)(2,1)S(1)}, bf16[64,1024]{1,0:T(8,128)(2,1)S(1)}, u32[]{:S(2)}, u32[]{:S(2)}) collective-permute-start(bf16[64,1024]{1,0:T(8,128)(2,1)S(1)} %convert_bitcast_fusion.own), channel_id=1, source_target_pairs={{0,2},{1,3},{2,0},{3,1},{4,6},{5,7},{6,4},{7,5},{8,10},{9,11},{10,... | collective-permute-start | bytes 393224 | tf_op jit(solution)/shard_map/ppermute | solution.py:437
  31.6 2.2 %collective-permute-start = (bf16[64,1024]{1,0:T(8,128)(2,1)S(1)}, bf16[64,1024]{1,0:T(8,128)(2,1)S(1)}, u32[]{:S(2)}, u32[]{:S(2)}) collective-permute-start(bf16[64,1024]{1,0:T(8,128)(2,1)S(1)} %convert_bitcast_fusion.own), channel_id=1, source_target_pairs={{0,1},{1,0},{2,3},{3,2},{4,5},{5,4},{6,7},{7,6},{8,9},{9,8},{10,11... | collective-permute-start | bytes 393224 | tf_op jit(solution)/shard_map/ppermute | solution.py:437
  33.8 0.0 collective-permute-done.2.next_3
  33.8 2.9 %collective-permute-done.1.next_2 = bf16[64,1024]{1,0:T(8,128)(2,1)S(1)} collective-permute-done((bf16[64,1024]{1,0:T(8,128)(2,1)S(1)}, bf16[64,1024]{1,0:T(8,128)(2,1)S(1)}, u32[]{:S(2)}, u32[]{:S(2)}) %collective-permute-start.1) | collective-permute-done | bytes 131104 | tf_op jit(solution)/shard_map/ppermute | solution.py:437
  36.7 0.9 collective-permute-done.next_1
  37.6 0.0 copy-start.1
  37.6 1.0 copy-done.1
  38.6 0.0 copy-start.2
  38.6 0.9 copy-done.2
  39.6 0.0 copy-start.3
  39.6 0.9 copy-done.3
  40.5 0.1 keep.1
  40.6 5.9 %all-to-all-done = bf16[128,5,2,128]{3,2,1,0:T(2,128)(2,1)S(1)} async-done(((bf16[128,5,2,128]{3,2,1,0:T(2,128)(2,1)}), bf16[128,5,2,128]{3,2,1,0:T(2,128)(2,1)S(1)}, u32[]{:S(2)}, u32[]{:S(2)}) %all-to-all-start) | async-done | bytes 327712 | tf_op jit(solution)/shard_map/all_to_all | solution.py:428
  46.5 10.8 %fit.1 = (f32[8192,256]{1,0:T(8,128)S(1)}, f32[128,128]{1,0:T(8,128)S(1)}, s32[2,8,128]{2,1,0:T(8,128)S(1)}) custom-call(bf16[1280,128]{1,0:T(8,128)(2,1)S(1)} %bitcast.15, bf16[256,1024]{1,0:T(8,128)(2,1)S(1)} %get-tuple-element.13.template, bf16[1312,112]{1,0:T(8,128)(2,1)S(1)} %get-tuple-element.14.band, bf16[160,768]{1,0:T(8,128)(2,1)S(1)} %get-tuple-element.15.wide_p, ...), custom_call_target="tpu_custom_call" | custom-call | tf_op jit(solution)/shard_map/fit/pallas_call | solution.py:376
  57.3 11.2 %all_to_all.25.parts = f32[8,16,128]{2,1,0:T(8,128)S(1)} all-to-all(f32[8,16,128]{2,1,0:T(8,128)S(1)} %bitcast.19), channel_id=1, replica_groups={{0,4,8,12,16,20,24,28},{32,36,40,44,48,52,56,60},{64,68,72,76,80,84,88,..., dimensions={0} | all-to-all | bytes 131072 | tf_op jit(solution)/shard_map/all_to_all | solution.py:428
  68.6 17.1 %all_to_all.26.parts = f32[16,16,128]{2,1,0:T(8,128)S(1)} all-to-all(f32[16,16,128]{2,1,0:T(8,128)S(1)} %middle.1), channel_id=1, replica_groups={{0,32,64,96,128,160,192,224,256,288,320,352,384,416,448,480},{4,36,68,1..., dimensions={0} | all-to-all | bytes 262144 | tf_op jit(solution)/shard_map/all_to_all | solution.py:428
  85.7 2.5 %solve.1 = f32[8,1,128]{2,1,0:T(1,128)S(1)} custom-call(f32[16,16,128]{2,1,0:T(8,128)S(1)} %all_to_all.26.parts), custom_call_target="tpu_custom_call" | custom-call | tf_op jit(solution)/shard_map/solve/pallas_call | solution.py:401
  88.2 10.8 %all_to_all.27 = f32[8,1,128]{2,1,0:T(1,128)S(1)} all-to-all(f32[8,1,128]{2,1,0:T(1,128)S(1)} %solve.1), channel_id=1, replica_groups={{0,4,8,12,16,20,24,28},{32,36,40,44,48,52,56,60},{64,68,72,76,80,84,88,..., dimensions={0} | all-to-all | bytes 8192 | tf_op jit(solution)/shard_map/all_to_all | solution.py:428
  98.9 2.5 %model.1 = bf16[512,128]{1,0:T(8,128)(2,1)} custom-call(s32[2,8,128]{2,1,0:T(8,128)S(1)} %get-tuple-element.17.details, f32[8,128]{1,0:T(8,128)S(1)} %bitcast.20, f32[8192,256]{1,0:T(8,128)S(1)} %get-tuple-element.19.images), custom_call_target="tpu_custom_call" | custom-call | tf_op jit(solution)/shard_map/model/pallas_call | solution.py:406
  101.4 6.2 %all-to-all-start.4 = ((bf16[128,2,2,128]{3,2,1,0:T(2,128)(2,1)}), bf16[128,2,2,128]{3,2,1,0:T(2,128)(2,1)S(1)}, u32[]{:S(2)}, u32[]{:S(2)}) async-start(bf16[128,2,2,128]{3,2,1,0:T(2,128)(2,1)} %bitcast.11), calls=%async_computation.4 | async-start | bytes 262144 | tf_op jit(solution)/shard_map/all_to_all | solution.py:428
  107.7 0.8 order.1
  108.5 15.2 %all-to-all-done.4 = bf16[128,2,2,128]{3,2,1,0:T(2,128)(2,1)S(1)} async-done(((bf16[128,2,2,128]{3,2,1,0:T(2,128)(2,1)}), bf16[128,2,2,128]{3,2,1,0:T(2,128)(2,1)S(1)}, u32[]{:S(2)}, u32[]{:S(2)}) %all-to-all-start.4) | async-done | bytes 131104 | tf_op jit(solution)/shard_map/all_to_all | solution.py:428
  123.7 0.0 copy-done
  123.7 0.0 copy-done.4
  123.7 0.9 final.1
  (1 shorter events, 0.0 us)
Async XLA Ops:
  0.6 123.1 %copy-start = (f32[128,2,128]{2,1,0:T(2,128)S(1)}, f32[128,2,128]{2,1,0:T(2,128)}, u32[]{:S(2)}) copy-start(f32[128,2,128]{2,1,0:T(2,128)} %param.9) | copy-start | bytes 393220
  3.1 120.6 %copy-start.4 = (s32[8,128]{1,0:T(8,128)S(1)}, s32[8,128]{1,0:T(8,128)}, u32[]{:S(2)}) copy-start(s32[8,128]{1,0:T(8,128)} %get-tuple-element.11.slots) | copy-start | bytes 12292
  3.1 43.4 %all-to-all-start = ((bf16[128,5,2,128]{3,2,1,0:T(2,128)(2,1)}), bf16[128,5,2,128]{3,2,1,0:T(2,128)(2,1)S(1)}, u32[]{:S(2)}, u32[]{:S(2)}) async-start(bf16[128,5,2,128]{3,2,1,0:T(2,128)(2,1)} %bitcast.22), calls=%async_computation | async-start | bytes 655360 | tf_op jit(solution)/shard_map/all_to_all | solution.py:428
  24.8 9.0 %collective-permute-start.2 = (bf16[64,1024]{1,0:T(8,128)(2,1)S(1)}, bf16[64,1024]{1,0:T(8,128)(2,1)S(1)}, u32[]{:S(2)}, u32[]{:S(2)}) collective-permute-start(bf16[64,1024]{1,0:T(8,128)(2,1)S(1)} %convert_bitcast_fusion.own), channel_id=1, source_target_pairs={{0,3},{1,2},{2,1},{3,0},{4,7},{5,6},{6,5},{7,4},{8,11},{9,10},{10,... | collective-permute-start | bytes 393224 | tf_op jit(solution)/shard_map/ppermute | solution.py:437
  29.2 7.5 %collective-permute-start.1 = (bf16[64,1024]{1,0:T(8,128)(2,1)S(1)}, bf16[64,1024]{1,0:T(8,128)(2,1)S(1)}, u32[]{:S(2)}, u32[]{:S(2)}) collective-permute-start(bf16[64,1024]{1,0:T(8,128)(2,1)S(1)} %convert_bitcast_fusion.own), channel_id=1, source_target_pairs={{0,2},{1,3},{2,0},{3,1},{4,6},{5,7},{6,4},{7,5},{8,10},{9,11},{10,... | collective-permute-start | bytes 393224 | tf_op jit(solution)/shard_map/ppermute | solution.py:437
  31.6 6.0 %collective-permute-start = (bf16[64,1024]{1,0:T(8,128)(2,1)S(1)}, bf16[64,1024]{1,0:T(8,128)(2,1)S(1)}, u32[]{:S(2)}, u32[]{:S(2)}) collective-permute-start(bf16[64,1024]{1,0:T(8,128)(2,1)S(1)} %convert_bitcast_fusion.own), channel_id=1, source_target_pairs={{0,1},{1,0},{2,3},{3,2},{4,5},{5,4},{6,7},{7,6},{8,9},{9,8},{10,11... | collective-permute-start | bytes 393224 | tf_op jit(solution)/shard_map/ppermute | solution.py:437
  37.6 1.0 copy-start.1
  38.6 0.9 copy-start.2
  39.6 0.9 copy-start.3
  101.4 22.2 %all-to-all-start.4 = ((bf16[128,2,2,128]{3,2,1,0:T(2,128)(2,1)}), bf16[128,2,2,128]{3,2,1,0:T(2,128)(2,1)S(1)}, u32[]{:S(2)}, u32[]{:S(2)}) async-start(bf16[128,2,2,128]{3,2,1,0:T(2,128)(2,1)} %bitcast.11), calls=%async_computation.4 | async-start | bytes 262144 | tf_op jit(solution)/shard_map/all_to_all | solution.py:428

commit v4 on v3

--- a/solution.py
+++ b/solution.py
@@ -16,6 +16,7 @@
 LANES = 128
 GROUP = 16
 DEPTH = 160
+SOLVE_BLOCK = 7
 FILTER_ROWS = 80
 FILTER_BAND = 656
 FILTER_DEPTH = 112
@@ -240,49 +241,69 @@
     accumulate(groups - 2, 0)
     combine(groups - 1, 1)
     accumulate(groups - 1, 1)
-    lane8 = iota((8, LANES), 1) >> 5
-    for v in range(VIS_DEV):
-        whole = total[v]
-        whole = whole + pltpu.roll(whole, 64, 1)
-        whole = whole + pltpu.roll(whole, 32, 1)
-        low = jnp.where(lane8 == 0, whole[0:8], whole[8:16])
-        high = jnp.where(lane8 == 2, whole[16:24], whole[24:32])
-        gram[v * 8 : v * 8 + 8, :] = jnp.where(lane8 < 2, low, high)
+    lane8 = iota((8, LANES), 1)
+    line = lane8[0:2] >> 5
+    for c in range(VIS_DEV // 2):
+        sums = []
+        for v in (2 * c, 2 * c + 1):
+            whole = total[v]
+            whole = whole + pltpu.roll(whole, 64, 1)
+            sums.append(whole + pltpu.roll(whole, 32, 1))
+        first, second = ([w[8 * p : 8 * p + 8] for p in range(4)] for w in sums)
+        upper = [jnp.where(lane8 < 64, x, y) for x, y in zip(first, second)]
+        place = lane8 & 63
+        main = jnp.where(place < 32, upper[0], upper[1])
+        gram[10 * c : 10 * c + 8, :] = jnp.where(
+            (place >= 32) & (place < 40),
+            jnp.where(lane8 < 64, pltpu.roll(first[3], 8, 1), pltpu.roll(second[3], 8, 1)), main)
+        extra = jnp.where((lane8 & 31) < 16, pltpu.roll(first[2], 16, 1), second[2])
+        low = jnp.where(line == 0, extra[0:2], extra[2:4])
+        high = jnp.where(line == 2, extra[4:6], extra[6:8])
+        gram[10 * c + 8 : 10 * c + 10, :] = jnp.where(line < 2, low, high)
+
+
+def total_of(parts):
+    main, extra = parts[0:8, :], parts[8:10, :]
+    for n in range(10, parts.shape[0], 10):
+        main = main + parts[n : n + 8, :]
+        extra = extra + parts[n + 8 : n + 10, :]
+    return main, extra
 
 
 def middle_kernel(parts, out):
-    whole = parts[0]
-    for n in range(1, parts.shape[0]):
-        whole = whole + parts[n]
-    for n in range(out.shape[0]):
-        out[n] = whole
+    main, extra = total_of(parts)
+    for n in range(0, out.shape[0], 10):
+        out[n : n + 8, :] = main
+        out[n + 8 : n + 10, :] = extra
 
 
 def solve_kernel(parts, out):
-    whole = parts[0]
-    for n in range(1, parts.shape[0]):
-        whole = whole + parts[n]
-    lane8 = iota((8, LANES), 1) >> 5
+    main, extra = total_of(parts)
+    rest = jnp.concatenate([extra if m == 0 else pltpu.roll(extra, 128 - 32 * m, 1) for m in range(4)], axis=0)
+    lane8 = iota((8, LANES), 1)
+    turns = ((main, 0, 96), (main, 96, 64), (rest, 16, 32), (main, 120, 88))
     pieces = []
-    for p in range(4):
-        piece = jnp.zeros((8, LANES), jnp.float32)
-        for h in range(2):
-            turned = whole[h * 8 : h * 8 + 8]
-            shift = (32 * h - 32 * p) % LANES
-            if shift:
-                turned = pltpu.roll(turned, shift, 1)
-            piece = jnp.where(lane8 == h, turned, piece)
-        pieces.append(piece)
+    for p, (source, near, far) in enumerate(turns):
+        near = pltpu.roll(source, near, 1) if near else source
+        piece = jnp.where(lane8 < 32, near, pltpu.roll(source, far, 1))
+        pieces.append(jnp.where((lane8 < 64) & ((lane8 & 31) >= 8 * p), piece, 0.0))
     matrix = jnp.concatenate(pieces, axis=0)
     lane = iota((ROWS, LANES), 1)
+    half = lane < 32
+    turned = jnp.concatenate([matrix, jnp.zeros((LANES - ROWS, LANES), jnp.float32)], axis=0).T
+    turned = jnp.where(half, turned[0:ROWS], pltpu.roll(turned[ROWS : 2 * ROWS], 32, 1))
+    below = (lane < 64) & (((lane & 31) >> 3) < (iota((ROWS, LANES), 0) >> 3))
+    matrix = jnp.where(below, turned, matrix)
     row_lane = iota((1, LANES), 1)
-    half = lane < 32
-    for k in basis_rows():
-        row = matrix[k : k + 1, :]
-        column = jnp.where(half, matrix[:, k : k + 1], matrix[:, 32 + k : 33 + k])
-        pivot = jnp.broadcast_to(column[k : k + 1, :], (ROWS, LANES))
-        scaled = column / pivot
-        matrix = jnp.where((lane & 31) == k, scaled, matrix - scaled * row)
+    order = basis_rows()
+    for start in range(0, len(order), SOLVE_BLOCK):
+        block = order[start : start + SOLVE_BLOCK]
+        columns = [jnp.where(half, matrix[:, k : k + 1], matrix[:, 32 + k : 33 + k]) for k in block]
+        for j, k in enumerate(block):
+            scaled = columns[j] / jnp.broadcast_to(columns[j][k : k + 1, :], (ROWS, LANES))
+            for i in range(j + 1, len(block)):
+                columns[i] = columns[i] - scaled * columns[i][k : k + 1, :]
+            matrix = jnp.where((lane & 31) == k, scaled, matrix - scaled * matrix[k : k + 1, :])
     answer = matrix[SCIENCE_ROW : SCIENCE_ROW + 1, :]
     valid = row_lane < 0
     for k in basis_rows():
@@ -375,7 +396,7 @@
 def fit(arrived, template, band, wide_p, wide_q):
     return pl.pallas_call(
         fit_kernel,
-        out_shape=(shape((2 * LANES * ROWS, 2 * LANES)), shape((VIS_DEV * 8, LANES)),
+        out_shape=(shape((2 * LANES * ROWS, 2 * LANES)), shape((VIS_DEV * 5, LANES)),
                    shape((2, 8, LANES), jnp.int32)),
         in_specs=vmem(5), out_specs=tuple(vmem(3)),
         scratch_shapes=[
@@ -393,7 +414,7 @@
 
 
 def middle(parts):
-    return pl.pallas_call(middle_kernel, out_shape=shape((16,) + parts.shape[1:]),
+    return pl.pallas_call(middle_kernel, out_shape=shape((2 * parts.shape[0], LANES)),
                           in_specs=vmem(1), out_specs=vmem(1)[0], compiler_params=params(4), name="middle")(parts)
 
 
@@ -442,8 +463,8 @@
     kept = keep(place, parts, constants())
     arrived = exchange(packed.reshape(patches, 5, 2, LANES)).reshape(LANES * SLOT_ROWS, LANES)
     images, gram, details = fit(arrived, *kept)
-    parts = exchange(gram.reshape(8, 16, LANES), planes)
-    parts = exchange(middle(parts), lines)
+    parts = exchange(gram.reshape(8, 5, 2, LANES), planes).reshape(gram.shape)
+    parts = exchange(middle(parts).reshape(16, 5, 2, LANES), lines).reshape(160, LANES)
     answers = exchange(solve(parts), planes).reshape(8, LANES)
     model = model_of(details, answers, images)
     returned = exchange(model.reshape(patches, 2, 2, LANES)).reshape(4 * LANES, LANES)

time: 125 us -> 122 us (0.976)
  blocking collectives: 39.1 us -> 37.4 us
    all_to_all x3, blocking collectives: 39.1 us -> 37.4 us  [exchange(): lax.all_to_all(values, 'patch', split_axis=0, concat_axis=0, tiled=True,...]
    pallas_call x1, Pallas kernels: 2.46 us -> 0.95 us  [solve(): pl.pallas_call(solve_kernel, out_shape=shape((8, 1, LANES)), in_specs=vme...]
where the time goes in v4:
time: 122 us; the launch traced here: 121 us
  blocking collectives  37.4 us (31%)
  starting transfers between devices  35.5 us (29%)
  waiting for transfers between devices  25.1 us (21%)
  Pallas kernels  19 us (16%)
  local copies, waits for them, and re-layouts  2.86 us (2%)
    all_to_all x3, blocking collectives, exchange(): lax.all_to_all(values, 'patch', split_axis=0, concat_axis=0, tiled=True,...  37.4 us
    all_to_all x2, starting transfers between devices, exchange(): lax.all_to_all(values, 'patch', split_axis=0, concat_axis=0, tiled=True,...  26.5 us
    all_to_all x2, waiting for transfers between devices, exchange(): lax.all_to_all(values, 'patch', split_axis=0, concat_axis=0, tiled=True,...  21.3 us
    pallas_call x1, Pallas kernels, fit(): pl.pallas_call(fit_kernel, out_shape=(shape((2 * LANES * ROWS, 2 * LANES)...  11.2 us
    ppermute x3, starting transfers between devices, per_device(): lax.ppermute(own, 'visit', [(x, x ^ m) for x in range(4)])  8.98 us
    ppermute x3, waiting for transfers between devices, per_device(): lax.ppermute(own, 'visit', [(x, x ^ m) for x in range(4)])  3.82 us
    unnamed x10, local copies, waits for them, and re-layouts  2.86 us
    pallas_call x1, Pallas kernels, model_of(): pl.pallas_call(model_kernel, out_shape=shape((4 * LANES, LANES), jnp.bflo...  2.5 us
  transfers between devices with their start and end apart: 5, of which 4 were waited for; matrix products, arithmetic and copies ran while one was open for 1% of the time, Pallas kernels for 1%

profile of v4, /device:TPU:1, one launch (start us, length us, event | category | flops | bytes accessed | tf_op | source)
XLA Modules:
  0.0 121.5 jit_solution(3150067775622769419)
XLA Ops:
  0.6 0.0 copy-start
  0.6 2.5 %pack.1 = (bf16[1280,128]{1,0:T(8,128)(2,1)}, s32[8,128]{1,0:T(8,128)}) custom-call(f32[256,128]{1,0:T(8,128)} %bitcast.19, f32[256,128]{1,0:T(8,128)} %bitcast.30, s32[1,128]{1,0:T(1,128)} %bitcast.32, s32[1,128]{1,0:T(1,128)} %bitcast.33, s32[2,128]{1,0:T(2,128)} %bitcast.31), custom_call_target="tpu_custom_call" | custom-call | tf_op jit(solution)/shard_map/pack/pallas_call | solution.py:378
  3.1 0.0 copy-start.4
  3.1 20.7 %all-to-all-start = ((bf16[128,5,2,128]{3,2,1,0:T(2,128)(2,1)}), bf16[128,5,2,128]{3,2,1,0:T(2,128)(2,1)S(1)}, u32[]{:S(2)}, u32[]{:S(2)}) async-start(bf16[128,5,2,128]{3,2,1,0:T(2,128)(2,1)} %bitcast.28), calls=%async_computation | async-start | bytes 655360 | tf_op jit(solution)/shard_map/all_to_all | solution.py:449
  23.8 1.0 convert_bitcast_fusion.own
  24.8 4.4 %collective-permute-start.2 = (bf16[64,1024]{1,0:T(8,128)(2,1)S(1)}, bf16[64,1024]{1,0:T(8,128)(2,1)S(1)}, u32[]{:S(2)}, u32[]{:S(2)}) collective-permute-start(bf16[64,1024]{1,0:T(8,128)(2,1)S(1)} %convert_bitcast_fusion.own), channel_id=1, source_target_pairs={{0,3},{1,2},{2,1},{3,0},{4,7},{5,6},{6,5},{7,4},{8,11},{9,10},{10,... | collective-permute-start | bytes 393224 | tf_op jit(solution)/shard_map/ppermute | solution.py:458
  29.2 2.4 %collective-permute-start.1 = (bf16[64,1024]{1,0:T(8,128)(2,1)S(1)}, bf16[64,1024]{1,0:T(8,128)(2,1)S(1)}, u32[]{:S(2)}, u32[]{:S(2)}) collective-permute-start(bf16[64,1024]{1,0:T(8,128)(2,1)S(1)} %convert_bitcast_fusion.own), channel_id=1, source_target_pairs={{0,2},{1,3},{2,0},{3,1},{4,6},{5,7},{6,4},{7,5},{8,10},{9,11},{10,... | collective-permute-start | bytes 393224 | tf_op jit(solution)/shard_map/ppermute | solution.py:458
  31.6 2.2 %collective-permute-start = (bf16[64,1024]{1,0:T(8,128)(2,1)S(1)}, bf16[64,1024]{1,0:T(8,128)(2,1)S(1)}, u32[]{:S(2)}, u32[]{:S(2)}) collective-permute-start(bf16[64,1024]{1,0:T(8,128)(2,1)S(1)} %convert_bitcast_fusion.own), channel_id=1, source_target_pairs={{0,1},{1,0},{2,3},{3,2},{4,5},{5,4},{6,7},{7,6},{8,9},{9,8},{10,11... | collective-permute-start | bytes 393224 | tf_op jit(solution)/shard_map/ppermute | solution.py:458
  33.8 0.0 collective-permute-done.2.next_3
  33.8 2.9 %collective-permute-done.1.next_2 = bf16[64,1024]{1,0:T(8,128)(2,1)S(1)} collective-permute-done((bf16[64,1024]{1,0:T(8,128)(2,1)S(1)}, bf16[64,1024]{1,0:T(8,128)(2,1)S(1)}, u32[]{:S(2)}, u32[]{:S(2)}) %collective-permute-start.1) | collective-permute-done | bytes 131104 | tf_op jit(solution)/shard_map/ppermute | solution.py:458
  36.7 0.9 collective-permute-done.next_1
  37.6 0.0 copy-start.1
  37.6 1.0 copy-done.1
  38.6 0.0 copy-start.2
  38.6 0.9 copy-done.2
  39.6 0.0 copy-start.3
  39.6 0.9 copy-done.3
  40.5 0.1 keep.1
  40.6 5.9 %all-to-all-done = bf16[128,5,2,128]{3,2,1,0:T(2,128)(2,1)S(1)} async-done(((bf16[128,5,2,128]{3,2,1,0:T(2,128)(2,1)}), bf16[128,5,2,128]{3,2,1,0:T(2,128)(2,1)S(1)}, u32[]{:S(2)}, u32[]{:S(2)}) %all-to-all-start) | async-done | bytes 327712 | tf_op jit(solution)/shard_map/all_to_all | solution.py:449
  46.5 11.2 %fit.1 = (f32[8192,256]{1,0:T(8,128)S(1)}, f32[80,128]{1,0:T(8,128)S(1)}, s32[2,8,128]{2,1,0:T(8,128)S(1)}) custom-call(bf16[1280,128]{1,0:T(8,128)(2,1)S(1)} %bitcast.18, bf16[256,1024]{1,0:T(8,128)(2,1)S(1)} %get-tuple-element.13.template, bf16[1312,112]{1,0:T(8,128)(2,1)S(1)} %get-tuple-element.14.band, bf16[160,768]{1,0:T(8,128)(2,1)S(1)} %get-tuple-element.15.wide_p, ...), custom_call_target="tpu_custom_call" | custom-call | tf_op jit(solution)/shard_map/fit/pallas_call | solution.py:397
  57.7 11.2 %all_to_all.25 = f32[8,5,2,128]{3,2,1,0:T(2,128)S(1)} all-to-all(f32[8,5,2,128]{3,2,1,0:T(2,128)S(1)} %bitcast.25), channel_id=1, replica_groups={{0,4,8,12,16,20,24,28},{32,36,40,44,48,52,56,60},{64,68,72,76,80,84,88,..., dimensions={0} | all-to-all | bytes 81920 | tf_op jit(solution)/shard_map/all_to_all | solution.py:449
  68.9 16.9 %all_to_all.26 = f32[16,5,2,128]{3,2,1,0:T(2,128)S(1)} all-to-all(f32[16,5,2,128]{3,2,1,0:T(2,128)S(1)} %bitcast.22), channel_id=1, replica_groups={{0,32,64,96,128,160,192,224,256,288,320,352,384,416,448,480},{4,36,68,1..., dimensions={0} | all-to-all | bytes 163840 | tf_op jit(solution)/shard_map/all_to_all | solution.py:449
  85.8 0.9 solve.1
  86.8 9.3 %all_to_all.27 = f32[8,1,128]{2,1,0:T(1,128)S(1)} all-to-all(f32[8,1,128]{2,1,0:T(1,128)S(1)} %solve.1), channel_id=1, replica_groups={{0,4,8,12,16,20,24,28},{32,36,40,44,48,52,56,60},{64,68,72,76,80,84,88,..., dimensions={0} | all-to-all | bytes 8192 | tf_op jit(solution)/shard_map/all_to_all | solution.py:449
  96.0 2.5 %model.1 = bf16[512,128]{1,0:T(8,128)(2,1)} custom-call(s32[2,8,128]{2,1,0:T(8,128)S(1)} %get-tuple-element.17.details, f32[8,128]{1,0:T(8,128)S(1)} %bitcast.26, f32[8192,256]{1,0:T(8,128)S(1)} %get-tuple-element.19.images), custom_call_target="tpu_custom_call" | custom-call | tf_op jit(solution)/shard_map/model/pallas_call | solution.py:427
  98.5 5.9 %all-to-all-start.4 = ((bf16[128,2,2,128]{3,2,1,0:T(2,128)(2,1)}), bf16[128,2,2,128]{3,2,1,0:T(2,128)(2,1)S(1)}, u32[]{:S(2)}, u32[]{:S(2)}) async-start(bf16[128,2,2,128]{3,2,1,0:T(2,128)(2,1)} %bitcast.14), calls=%async_computation.4 | async-start | bytes 262144 | tf_op jit(solution)/shard_map/all_to_all | solution.py:449
  104.4 0.8 order.1
  105.2 15.3 %all-to-all-done.4 = bf16[128,2,2,128]{3,2,1,0:T(2,128)(2,1)S(1)} async-done(((bf16[128,2,2,128]{3,2,1,0:T(2,128)(2,1)}), bf16[128,2,2,128]{3,2,1,0:T(2,128)(2,1)S(1)}, u32[]{:S(2)}, u32[]{:S(2)}) %all-to-all-start.4) | async-done | bytes 131104 | tf_op jit(solution)/shard_map/all_to_all | solution.py:449
  120.6 0.0 copy-done
  120.6 0.0 copy-done.4
  120.6 0.9 final.1
  (1 shorter events, 0.0 us)
Async XLA Ops:
  0.6 119.9 %copy-start = (f32[128,2,128]{2,1,0:T(2,128)S(1)}, f32[128,2,128]{2,1,0:T(2,128)}, u32[]{:S(2)}) copy-start(f32[128,2,128]{2,1,0:T(2,128)} %param.9) | copy-start | bytes 393220
  3.1 117.4 %copy-start.4 = (s32[8,128]{1,0:T(8,128)S(1)}, s32[8,128]{1,0:T(8,128)}, u32[]{:S(2)}) copy-start(s32[8,128]{1,0:T(8,128)} %get-tuple-element.11.slots) | copy-start | bytes 12292
  3.1 43.4 %all-to-all-start = ((bf16[128,5,2,128]{3,2,1,0:T(2,128)(2,1)}), bf16[128,5,2,128]{3,2,1,0:T(2,128)(2,1)S(1)}, u32[]{:S(2)}, u32[]{:S(2)}) async-start(bf16[128,5,2,128]{3,2,1,0:T(2,128)(2,1)} %bitcast.28), calls=%async_computation | async-start | bytes 655360 | tf_op jit(solution)/shard_map/all_to_all | solution.py:449
  24.8 9.0 %collective-permute-start.2 = (bf16[64,1024]{1,0:T(8,128)(2,1)S(1)}, bf16[64,1024]{1,0:T(8,128)(2,1)S(1)}, u32[]{:S(2)}, u32[]{:S(2)}) collective-permute-start(bf16[64,1024]{1,0:T(8,128)(2,1)S(1)} %convert_bitcast_fusion.own), channel_id=1, source_target_pairs={{0,3},{1,2},{2,1},{3,0},{4,7},{5,6},{6,5},{7,4},{8,11},{9,10},{10,... | collective-permute-start | bytes 393224 | tf_op jit(solution)/shard_map/ppermute | solution.py:458
  29.2 7.5 %collective-permute-start.1 = (bf16[64,1024]{1,0:T(8,128)(2,1)S(1)}, bf16[64,1024]{1,0:T(8,128)(2,1)S(1)}, u32[]{:S(2)}, u32[]{:S(2)}) collective-permute-start(bf16[64,1024]{1,0:T(8,128)(2,1)S(1)} %convert_bitcast_fusion.own), channel_id=1, source_target_pairs={{0,2},{1,3},{2,0},{3,1},{4,6},{5,7},{6,4},{7,5},{8,10},{9,11},{10,... | collective-permute-start | bytes 393224 | tf_op jit(solution)/shard_map/ppermute | solution.py:458
  31.6 6.0 %collective-permute-start = (bf16[64,1024]{1,0:T(8,128)(2,1)S(1)}, bf16[64,1024]{1,0:T(8,128)(2,1)S(1)}, u32[]{:S(2)}, u32[]{:S(2)}) collective-permute-start(bf16[64,1024]{1,0:T(8,128)(2,1)S(1)} %convert_bitcast_fusion.own), channel_id=1, source_target_pairs={{0,1},{1,0},{2,3},{3,2},{4,5},{5,4},{6,7},{7,6},{8,9},{9,8},{10,11... | collective-permute-start | bytes 393224 | tf_op jit(solution)/shard_map/ppermute | solution.py:458
  37.6 1.0 copy-start.1
  38.6 0.9 copy-start.2
  39.6 0.9 copy-start.3
  98.5 22.0 %all-to-all-start.4 = ((bf16[128,2,2,128]{3,2,1,0:T(2,128)(2,1)}), bf16[128,2,2,128]{3,2,1,0:T(2,128)(2,1)S(1)}, u32[]{:S(2)}, u32[]{:S(2)}) async-start(bf16[128,2,2,128]{3,2,1,0:T(2,128)(2,1)} %bitcast.14), calls=%async_computation.4 | async-start | bytes 262144 | tf_op jit(solution)/shard_map/all_to_all | solution.py:449

commit v5 on v4

--- a/solution.py
+++ b/solution.py
@@ -272,9 +272,9 @@
 
 def middle_kernel(parts, out):
     main, extra = total_of(parts)
-    for n in range(0, out.shape[0], 10):
-        out[n : n + 8, :] = main
-        out[n + 8 : n + 10, :] = extra
+    for n in range(4):
+        out[n] = main[2 * n : 2 * n + 2]
+    out[4] = extra
 
 
 def solve_kernel(parts, out):
@@ -414,7 +414,7 @@
 
 
 def middle(parts):
-    return pl.pallas_call(middle_kernel, out_shape=shape((2 * parts.shape[0], LANES)),
+    return pl.pallas_call(middle_kernel, out_shape=shape((5, 2, LANES)),
                           in_specs=vmem(1), out_specs=vmem(1)[0], compiler_params=params(4), name="middle")(parts)
 
 
@@ -464,7 +464,8 @@
     arrived = exchange(packed.reshape(patches, 5, 2, LANES)).reshape(LANES * SLOT_ROWS, LANES)
     images, gram, details = fit(arrived, *kept)
     parts = exchange(gram.reshape(8, 5, 2, LANES), planes).reshape(gram.shape)
-    parts = exchange(middle(parts).reshape(16, 5, 2, LANES), lines).reshape(160, LANES)
+    parts = lax.all_gather(middle(parts), "patch", axis_index_groups=lines)
+    parts = parts.reshape(160, LANES)
     answers = exchange(solve(parts), planes).reshape(8, LANES)
     model = model_of(details, answers, images)
     returned = exchange(model.reshape(patches, 2, 2, LANES)).reshape(4 * LANES, LANES)

time: 122 us -> 133 us (1.090)
  blocking collectives: 37.4 us -> 46.2 us
  starting transfers between devices: 35.5 us -> 37.4 us
    all_gather x0 -> x1, blocking collectives: none -> 20.4 us  [per_device(): parts = lax.all_gather(middle(parts), 'patch', axis_index_groups=lines)]
    all_to_all x3 -> x2, blocking collectives: 37.4 us -> 25.8 us  [exchange(): lax.all_to_all(values, 'patch', split_axis=0, concat_axis=0, tiled=True,...]
    all_to_all x2, starting transfers between devices: 26.5 us -> 28.4 us  [exchange(): lax.all_to_all(values, 'patch', split_axis=0, concat_axis=0, tiled=True,...]
where the time goes in v5:
time: 133 us; the launch traced here: 132 us
  blocking collectives  46.2 us (35%)
  starting transfers between devices  37.4 us (28%)
  waiting for transfers between devices  24.9 us (19%)
  Pallas kernels  19 us (14%)
  local copies, waits for them, and re-layouts  2.86 us (2%)
    all_to_all x2, starting transfers between devices, exchange(): lax.all_to_all(values, 'patch', split_axis=0, concat_axis=0, tiled=True,...  28.4 us
    all_to_all x2, blocking collectives, exchange(): lax.all_to_all(values, 'patch', split_axis=0, concat_axis=0, tiled=True,...  25.8 us
    all_to_all x2, waiting for transfers between devices, exchange(): lax.all_to_all(values, 'patch', split_axis=0, concat_axis=0, tiled=True,...  21.1 us
    all_gather x1, blocking collectives, per_device(): parts = lax.all_gather(middle(parts), 'patch', axis_index_groups=lines)  20.4 us
    pallas_call x1, Pallas kernels, fit(): pl.pallas_call(fit_kernel, out_shape=(shape((2 * LANES * ROWS, 2 * LANES)...  11.2 us
    ppermute x3, starting transfers between devices, per_device(): lax.ppermute(own, 'visit', [(x, x ^ m) for x in range(4)])  8.98 us
    ppermute x3, waiting for transfers between devices, per_device(): lax.ppermute(own, 'visit', [(x, x ^ m) for x in range(4)])  3.82 us
    unnamed x10, local copies, waits for them, and re-layouts  2.86 us
  transfers between devices with their start and end apart: 5, of which 4 were waited for; matrix products, arithmetic and copies ran while one was open for 1% of the time, Pallas kernels for 1%

profile of v5, /device:TPU:1, one launch (start us, length us, event | category | flops | bytes accessed | tf_op | source)
XLA Modules:
  0.0 132.1 jit_solution(5016318217942910516)
XLA Ops:
  0.6 0.0 copy-start
  0.6 2.5 %pack.1 = (bf16[1280,128]{1,0:T(8,128)(2,1)}, s32[8,128]{1,0:T(8,128)}) custom-call(f32[256,128]{1,0:T(8,128)} %bitcast.18, f32[256,128]{1,0:T(8,128)} %bitcast.28, s32[1,128]{1,0:T(1,128)} %bitcast.30, s32[1,128]{1,0:T(1,128)} %bitcast.31, s32[2,128]{1,0:T(2,128)} %bitcast.29), custom_call_target="tpu_custom_call" | custom-call | tf_op jit(solution)/shard_map/pack/pallas_call | solution.py:378
  3.1 0.0 copy-start.4
  3.1 20.7 %all-to-all-start = ((bf16[128,5,2,128]{3,2,1,0:T(2,128)(2,1)}), bf16[128,5,2,128]{3,2,1,0:T(2,128)(2,1)S(1)}, u32[]{:S(2)}, u32[]{:S(2)}) async-start(bf16[128,5,2,128]{3,2,1,0:T(2,128)(2,1)} %bitcast.26), calls=%async_computation | async-start | bytes 655360 | tf_op jit(solution)/shard_map/all_to_all | solution.py:449
  23.8 1.0 convert_bitcast_fusion.own
  24.8 4.4 %collective-permute-start.2 = (bf16[64,1024]{1,0:T(8,128)(2,1)S(1)}, bf16[64,1024]{1,0:T(8,128)(2,1)S(1)}, u32[]{:S(2)}, u32[]{:S(2)}) collective-permute-start(bf16[64,1024]{1,0:T(8,128)(2,1)S(1)} %convert_bitcast_fusion.own), channel_id=1, source_target_pairs={{0,3},{1,2},{2,1},{3,0},{4,7},{5,6},{6,5},{7,4},{8,11},{9,10},{10,... | collective-permute-start | bytes 393224 | tf_op jit(solution)/shard_map/ppermute | solution.py:458
  29.2 2.4 %collective-permute-start.1 = (bf16[64,1024]{1,0:T(8,128)(2,1)S(1)}, bf16[64,1024]{1,0:T(8,128)(2,1)S(1)}, u32[]{:S(2)}, u32[]{:S(2)}) collective-permute-start(bf16[64,1024]{1,0:T(8,128)(2,1)S(1)} %convert_bitcast_fusion.own), channel_id=1, source_target_pairs={{0,2},{1,3},{2,0},{3,1},{4,6},{5,7},{6,4},{7,5},{8,10},{9,11},{10,... | collective-permute-start | bytes 393224 | tf_op jit(solution)/shard_map/ppermute | solution.py:458
  31.6 2.2 %collective-permute-start = (bf16[64,1024]{1,0:T(8,128)(2,1)S(1)}, bf16[64,1024]{1,0:T(8,128)(2,1)S(1)}, u32[]{:S(2)}, u32[]{:S(2)}) collective-permute-start(bf16[64,1024]{1,0:T(8,128)(2,1)S(1)} %convert_bitcast_fusion.own), channel_id=1, source_target_pairs={{0,1},{1,0},{2,3},{3,2},{4,5},{5,4},{6,7},{7,6},{8,9},{9,8},{10,11... | collective-permute-start | bytes 393224 | tf_op jit(solution)/shard_map/ppermute | solution.py:458
  33.8 0.0 collective-permute-done.2.next_3
  33.8 2.9 %collective-permute-done.1.next_2 = bf16[64,1024]{1,0:T(8,128)(2,1)S(1)} collective-permute-done((bf16[64,1024]{1,0:T(8,128)(2,1)S(1)}, bf16[64,1024]{1,0:T(8,128)(2,1)S(1)}, u32[]{:S(2)}, u32[]{:S(2)}) %collective-permute-start.1) | collective-permute-done | bytes 131104 | tf_op jit(solution)/shard_map/ppermute | solution.py:458
  36.7 0.9 collective-permute-done.next_1
  37.6 0.0 copy-start.1
  37.6 1.0 copy-done.1
  38.6 0.0 copy-start.2
  38.6 0.9 copy-done.2
  39.6 0.0 copy-start.3
  39.6 0.9 copy-done.3
  40.5 0.1 keep.1
  40.6 5.9 %all-to-all-done = bf16[128,5,2,128]{3,2,1,0:T(2,128)(2,1)S(1)} async-done(((bf16[128,5,2,128]{3,2,1,0:T(2,128)(2,1)}), bf16[128,5,2,128]{3,2,1,0:T(2,128)(2,1)S(1)}, u32[]{:S(2)}, u32[]{:S(2)}) %all-to-all-start) | async-done | bytes 327712 | tf_op jit(solution)/shard_map/all_to_all | solution.py:449
  46.5 11.2 %fit.1 = (f32[8192,256]{1,0:T(8,128)S(1)}, f32[80,128]{1,0:T(8,128)S(1)}, s32[2,8,128]{2,1,0:T(8,128)S(1)}) custom-call(bf16[1280,128]{1,0:T(8,128)(2,1)S(1)} %bitcast.17, bf16[256,1024]{1,0:T(8,128)(2,1)S(1)} %get-tuple-element.13.template, bf16[1312,112]{1,0:T(8,128)(2,1)S(1)} %get-tuple-element.14.band, bf16[160,768]{1,0:T(8,128)(2,1)S(1)} %get-tuple-element.15.wide_p, ...), custom_call_target="tpu_custom_call" | custom-call | tf_op jit(solution)/shard_map/fit/pallas_call | solution.py:397
  57.7 11.2 %all_to_all.20 = f32[8,5,2,128]{3,2,1,0:T(2,128)S(1)} all-to-all(f32[8,5,2,128]{3,2,1,0:T(2,128)S(1)} %bitcast.23), channel_id=1, replica_groups={{0,4,8,12,16,20,24,28},{32,36,40,44,48,52,56,60},{64,68,72,76,80,84,88,..., dimensions={0} | all-to-all | bytes 81920 | tf_op jit(solution)/shard_map/all_to_all | solution.py:449
  68.9 20.4 %all-gather = f32[80,2,128]{2,1,0:T(2,128)S(1)} all-gather(f32[5,2,128]{2,1,0:T(2,128)S(1)} %middle.1), channel_id=2, replica_groups={{0,32,64,96,128,160,192,224,256,288,320,352,384,416,448,480},{4,36,68,1..., dimensions={0}, use_global_device_ids=true | all-gather | bytes 87040 | tf_op jit(solution)/shard_map/all_gather | solution.py:467
  89.3 0.9 solve.1
  90.2 14.7 %all_to_all.21 = f32[8,1,128]{2,1,0:T(1,128)S(1)} all-to-all(f32[8,1,128]{2,1,0:T(1,128)S(1)} %solve.1), channel_id=1, replica_groups={{0,4,8,12,16,20,24,28},{32,36,40,44,48,52,56,60},{64,68,72,76,80,84,88,..., dimensions={0} | all-to-all | bytes 8192 | tf_op jit(solution)/shard_map/all_to_all | solution.py:449
  104.9 2.5 %model.1 = bf16[512,128]{1,0:T(8,128)(2,1)} custom-call(s32[2,8,128]{2,1,0:T(8,128)S(1)} %get-tuple-element.17.details, f32[8,128]{1,0:T(8,128)S(1)} %bitcast.24, f32[8192,256]{1,0:T(8,128)S(1)} %get-tuple-element.19.images), custom_call_target="tpu_custom_call" | custom-call | tf_op jit(solution)/shard_map/model/pallas_call | solution.py:427
  107.4 7.7 %all-to-all-start.3 = ((bf16[128,2,2,128]{3,2,1,0:T(2,128)(2,1)}), bf16[128,2,2,128]{3,2,1,0:T(2,128)(2,1)S(1)}, u32[]{:S(2)}, u32[]{:S(2)}) async-start(bf16[128,2,2,128]{3,2,1,0:T(2,128)(2,1)} %bitcast.13), calls=%async_computation.3 | async-start | bytes 262144 | tf_op jit(solution)/shard_map/all_to_all | solution.py:449
  115.1 0.8 order.1
  116.0 15.2 %all-to-all-done.3 = bf16[128,2,2,128]{3,2,1,0:T(2,128)(2,1)S(1)} async-done(((bf16[128,2,2,128]{3,2,1,0:T(2,128)(2,1)}), bf16[128,2,2,128]{3,2,1,0:T(2,128)(2,1)S(1)}, u32[]{:S(2)}, u32[]{:S(2)}) %all-to-all-start.3) | async-done | bytes 131104 | tf_op jit(solution)/shard_map/all_to_all | solution.py:449
  131.1 0.0 copy-done
  131.1 0.0 copy-done.4
  131.1 0.9 final.1
  (1 shorter events, 0.0 us)
Async XLA Ops:
  0.6 130.5 %copy-start = (f32[128,2,128]{2,1,0:T(2,128)S(1)}, f32[128,2,128]{2,1,0:T(2,128)}, u32[]{:S(2)}) copy-start(f32[128,2,128]{2,1,0:T(2,128)} %param.9) | copy-start | bytes 393220
  3.1 128.0 %copy-start.4 = (s32[8,128]{1,0:T(8,128)S(1)}, s32[8,128]{1,0:T(8,128)}, u32[]{:S(2)}) copy-start(s32[8,128]{1,0:T(8,128)} %get-tuple-element.11.slots) | copy-start | bytes 12292
  3.1 43.4 %all-to-all-start = ((bf16[128,5,2,128]{3,2,1,0:T(2,128)(2,1)}), bf16[128,5,2,128]{3,2,1,0:T(2,128)(2,1)S(1)}, u32[]{:S(2)}, u32[]{:S(2)}) async-start(bf16[128,5,2,128]{3,2,1,0:T(2,128)(2,1)} %bitcast.26), calls=%async_computation | async-start | bytes 655360 | tf_op jit(solution)/shard_map/all_to_all | solution.py:449
  24.8 9.0 %collective-permute-start.2 = (bf16[64,1024]{1,0:T(8,128)(2,1)S(1)}, bf16[64,1024]{1,0:T(8,128)(2,1)S(1)}, u32[]{:S(2)}, u32[]{:S(2)}) collective-permute-start(bf16[64,1024]{1,0:T(8,128)(2,1)S(1)} %convert_bitcast_fusion.own), channel_id=1, source_target_pairs={{0,3},{1,2},{2,1},{3,0},{4,7},{5,6},{6,5},{7,4},{8,11},{9,10},{10,... | collective-permute-start | bytes 393224 | tf_op jit(solution)/shard_map/ppermute | solution.py:458
  29.2 7.5 %collective-permute-start.1 = (bf16[64,1024]{1,0:T(8,128)(2,1)S(1)}, bf16[64,1024]{1,0:T(8,128)(2,1)S(1)}, u32[]{:S(2)}, u32[]{:S(2)}) collective-permute-start(bf16[64,1024]{1,0:T(8,128)(2,1)S(1)} %convert_bitcast_fusion.own), channel_id=1, source_target_pairs={{0,2},{1,3},{2,0},{3,1},{4,6},{5,7},{6,4},{7,5},{8,10},{9,11},{10,... | collective-permute-start | bytes 393224 | tf_op jit(solution)/shard_map/ppermute | solution.py:458
  31.6 6.0 %collective-permute-start = (bf16[64,1024]{1,0:T(8,128)(2,1)S(1)}, bf16[64,1024]{1,0:T(8,128)(2,1)S(1)}, u32[]{:S(2)}, u32[]{:S(2)}) collective-permute-start(bf16[64,1024]{1,0:T(8,128)(2,1)S(1)} %convert_bitcast_fusion.own), channel_id=1, source_target_pairs={{0,1},{1,0},{2,3},{3,2},{4,5},{5,4},{6,7},{7,6},{8,9},{9,8},{10,11... | collective-permute-start | bytes 393224 | tf_op jit(solution)/shard_map/ppermute | solution.py:458
  37.6 1.0 copy-start.1
  38.6 0.9 copy-start.2
  39.6 0.9 copy-start.3
  107.4 23.7 %all-to-all-start.3 = ((bf16[128,2,2,128]{3,2,1,0:T(2,128)(2,1)}), bf16[128,2,2,128]{3,2,1,0:T(2,128)(2,1)S(1)}, u32[]{:S(2)}, u32[]{:S(2)}) async-start(bf16[128,2,2,128]{3,2,1,0:T(2,128)(2,1)} %bitcast.13), calls=%async_computation.3 | async-start | bytes 262144 | tf_op jit(solution)/shard_map/all_to_all | solution.py:449

commit v6 on v4

--- a/solution.py
+++ b/solution.py
@@ -14,7 +14,7 @@
 VIS_DEV = 16
 ROWS = 32
 LANES = 128
-GROUP = 16
+GROUP = 32
 DEPTH = 160
 SOLVE_BLOCK = 7
 FILTER_ROWS = 80

time: 122 us -> 121 us (level)
  no operation moved by 1% of the time
where the time goes in v6:
time: 121 us
  blocking collectives  37.4 us (31%)
  starting transfers between devices  35.5 us (29%)
  waiting for transfers between devices  25.1 us (21%)
  Pallas kernels  18.3 us (15%)
  local copies, waits for them, and re-layouts  2.86 us (2%)
    all_to_all x3, blocking collectives, exchange(): lax.all_to_all(values, 'patch', split_axis=0, concat_axis=0, tiled=True,...  37.4 us
    all_to_all x2, starting transfers between devices, exchange(): lax.all_to_all(values, 'patch', split_axis=0, concat_axis=0, tiled=True,...  26.5 us
    all_to_all x2, waiting for transfers between devices, exchange(): lax.all_to_all(values, 'patch', split_axis=0, concat_axis=0, tiled=True,...  21.3 us
    pallas_call x1, Pallas kernels, fit(): pl.pallas_call(fit_kernel, out_shape=(shape((2 * LANES * ROWS, 2 * LANES)...  10.5 us
    ppermute x3, starting transfers between devices, per_device(): lax.ppermute(own, 'visit', [(x, x ^ m) for x in range(4)])  8.98 us
    ppermute x3, waiting for transfers between devices, per_device(): lax.ppermute(own, 'visit', [(x, x ^ m) for x in range(4)])  3.82 us
    unnamed x10, local copies, waits for them, and re-layouts  2.86 us
    pallas_call x1, Pallas kernels, model_of(): pl.pallas_call(model_kernel, out_shape=shape((4 * LANES, LANES), jnp.bflo...  2.5 us
  transfers between devices with their start and end apart: 5, of which 4 were waited for; matrix products, arithmetic and copies ran while one was open for 1% of the time, Pallas kernels for 1%

profile of v6, /device:TPU:1, one launch (start us, length us, event | category | flops | bytes accessed | tf_op | source)
XLA Modules:
  0.0 120.9 jit_solution(15500462657537484558)
XLA Ops:
  0.6 0.0 copy-start
  0.6 2.5 %pack.1 = (bf16[1280,128]{1,0:T(8,128)(2,1)}, s32[8,128]{1,0:T(8,128)}) custom-call(f32[256,128]{1,0:T(8,128)} %bitcast.19, f32[256,128]{1,0:T(8,128)} %bitcast.30, s32[1,128]{1,0:T(1,128)} %bitcast.32, s32[1,128]{1,0:T(1,128)} %bitcast.33, s32[2,128]{1,0:T(2,128)} %bitcast.31), custom_call_target="tpu_custom_call" | custom-call | tf_op jit(solution)/shard_map/pack/pallas_call | solution.py:378
  3.1 0.0 copy-start.4
  3.1 20.7 %all-to-all-start = ((bf16[128,5,2,128]{3,2,1,0:T(2,128)(2,1)}), bf16[128,5,2,128]{3,2,1,0:T(2,128)(2,1)S(1)}, u32[]{:S(2)}, u32[]{:S(2)}) async-start(bf16[128,5,2,128]{3,2,1,0:T(2,128)(2,1)} %bitcast.28), calls=%async_computation | async-start | bytes 655360 | tf_op jit(solution)/shard_map/all_to_all | solution.py:449
  23.8 1.0 convert_bitcast_fusion.own
  24.8 4.4 %collective-permute-start.2 = (bf16[64,1024]{1,0:T(8,128)(2,1)S(1)}, bf16[64,1024]{1,0:T(8,128)(2,1)S(1)}, u32[]{:S(2)}, u32[]{:S(2)}) collective-permute-start(bf16[64,1024]{1,0:T(8,128)(2,1)S(1)} %convert_bitcast_fusion.own), channel_id=1, source_target_pairs={{0,3},{1,2},{2,1},{3,0},{4,7},{5,6},{6,5},{7,4},{8,11},{9,10},{10,... | collective-permute-start | bytes 393224 | tf_op jit(solution)/shard_map/ppermute | solution.py:458
  29.2 2.4 %collective-permute-start.1 = (bf16[64,1024]{1,0:T(8,128)(2,1)S(1)}, bf16[64,1024]{1,0:T(8,128)(2,1)S(1)}, u32[]{:S(2)}, u32[]{:S(2)}) collective-permute-start(bf16[64,1024]{1,0:T(8,128)(2,1)S(1)} %convert_bitcast_fusion.own), channel_id=1, source_target_pairs={{0,2},{1,3},{2,0},{3,1},{4,6},{5,7},{6,4},{7,5},{8,10},{9,11},{10,... | collective-permute-start | bytes 393224 | tf_op jit(solution)/shard_map/ppermute | solution.py:458
  31.6 2.2 %collective-permute-start = (bf16[64,1024]{1,0:T(8,128)(2,1)S(1)}, bf16[64,1024]{1,0:T(8,128)(2,1)S(1)}, u32[]{:S(2)}, u32[]{:S(2)}) collective-permute-start(bf16[64,1024]{1,0:T(8,128)(2,1)S(1)} %convert_bitcast_fusion.own), channel_id=1, source_target_pairs={{0,1},{1,0},{2,3},{3,2},{4,5},{5,4},{6,7},{7,6},{8,9},{9,8},{10,11... | collective-permute-start | bytes 393224 | tf_op jit(solution)/shard_map/ppermute | solution.py:458
  33.8 0.0 collective-permute-done.2.next_3
  33.8 2.9 %collective-permute-done.1.next_2 = bf16[64,1024]{1,0:T(8,128)(2,1)S(1)} collective-permute-done((bf16[64,1024]{1,0:T(8,128)(2,1)S(1)}, bf16[64,1024]{1,0:T(8,128)(2,1)S(1)}, u32[]{:S(2)}, u32[]{:S(2)}) %collective-permute-start.1) | collective-permute-done | bytes 131104 | tf_op jit(solution)/shard_map/ppermute | solution.py:458
  36.7 0.9 collective-permute-done.next_1
  37.6 0.0 copy-start.1
  37.6 1.0 copy-done.1
  38.6 0.0 copy-start.2
  38.6 0.9 copy-done.2
  39.6 0.0 copy-start.3
  39.6 0.9 copy-done.3
  40.5 0.1 keep.1
  40.6 5.9 %all-to-all-done = bf16[128,5,2,128]{3,2,1,0:T(2,128)(2,1)S(1)} async-done(((bf16[128,5,2,128]{3,2,1,0:T(2,128)(2,1)}), bf16[128,5,2,128]{3,2,1,0:T(2,128)(2,1)S(1)}, u32[]{:S(2)}, u32[]{:S(2)}) %all-to-all-start) | async-done | bytes 327712 | tf_op jit(solution)/shard_map/all_to_all | solution.py:449
  46.5 10.5 %fit.1 = (f32[8192,256]{1,0:T(8,128)S(1)}, f32[80,128]{1,0:T(8,128)S(1)}, s32[2,8,128]{2,1,0:T(8,128)S(1)}) custom-call(bf16[1280,128]{1,0:T(8,128)(2,1)S(1)} %bitcast.18, bf16[256,1024]{1,0:T(8,128)(2,1)S(1)} %get-tuple-element.13.template, bf16[1312,112]{1,0:T(8,128)(2,1)S(1)} %get-tuple-element.14.band, bf16[160,768]{1,0:T(8,128)(2,1)S(1)} %get-tuple-element.15.wide_p, ...), custom_call_target="tpu_custom_call" | custom-call | tf_op jit(solution)/shard_map/fit/pallas_call | solution.py:397
  57.0 11.1 %all_to_all.25 = f32[8,5,2,128]{3,2,1,0:T(2,128)S(1)} all-to-all(f32[8,5,2,128]{3,2,1,0:T(2,128)S(1)} %bitcast.25), channel_id=1, replica_groups={{0,4,8,12,16,20,24,28},{32,36,40,44,48,52,56,60},{64,68,72,76,80,84,88,..., dimensions={0} | all-to-all | bytes 81920 | tf_op jit(solution)/shard_map/all_to_all | solution.py:449
  68.2 17.0 %all_to_all.26 = f32[16,5,2,128]{3,2,1,0:T(2,128)S(1)} all-to-all(f32[16,5,2,128]{3,2,1,0:T(2,128)S(1)} %bitcast.22), channel_id=1, replica_groups={{0,32,64,96,128,160,192,224,256,288,320,352,384,416,448,480},{4,36,68,1..., dimensions={0} | all-to-all | bytes 163840 | tf_op jit(solution)/shard_map/all_to_all | solution.py:449
  85.2 0.9 solve.1
  86.2 9.3 %all_to_all.27 = f32[8,1,128]{2,1,0:T(1,128)S(1)} all-to-all(f32[8,1,128]{2,1,0:T(1,128)S(1)} %solve.1), channel_id=1, replica_groups={{0,4,8,12,16,20,24,28},{32,36,40,44,48,52,56,60},{64,68,72,76,80,84,88,..., dimensions={0} | all-to-all | bytes 8192 | tf_op jit(solution)/shard_map/all_to_all | solution.py:449
  95.4 2.5 %model.1 = bf16[512,128]{1,0:T(8,128)(2,1)} custom-call(s32[2,8,128]{2,1,0:T(8,128)S(1)} %get-tuple-element.17.details, f32[8,128]{1,0:T(8,128)S(1)} %bitcast.26, f32[8192,256]{1,0:T(8,128)S(1)} %get-tuple-element.19.images), custom_call_target="tpu_custom_call" | custom-call | tf_op jit(solution)/shard_map/model/pallas_call | solution.py:427
  97.9 5.9 %all-to-all-start.4 = ((bf16[128,2,2,128]{3,2,1,0:T(2,128)(2,1)}), bf16[128,2,2,128]{3,2,1,0:T(2,128)(2,1)S(1)}, u32[]{:S(2)}, u32[]{:S(2)}) async-start(bf16[128,2,2,128]{3,2,1,0:T(2,128)(2,1)} %bitcast.14), calls=%async_computation.4 | async-start | bytes 262144 | tf_op jit(solution)/shard_map/all_to_all | solution.py:449
  103.8 0.8 order.1
  104.6 15.3 %all-to-all-done.4 = bf16[128,2,2,128]{3,2,1,0:T(2,128)(2,1)S(1)} async-done(((bf16[128,2,2,128]{3,2,1,0:T(2,128)(2,1)}), bf16[128,2,2,128]{3,2,1,0:T(2,128)(2,1)S(1)}, u32[]{:S(2)}, u32[]{:S(2)}) %all-to-all-start.4) | async-done | bytes 131104 | tf_op jit(solution)/shard_map/all_to_all | solution.py:449
  120.0 0.0 copy-done
  120.0 0.0 copy-done.4
  120.0 0.9 final.1
  (1 shorter events, 0.0 us)
Async XLA Ops:
  0.6 119.3 %copy-start = (f32[128,2,128]{2,1,0:T(2,128)S(1)}, f32[128,2,128]{2,1,0:T(2,128)}, u32[]{:S(2)}) copy-start(f32[128,2,128]{2,1,0:T(2,128)} %param.9) | copy-start | bytes 393220
  3.1 116.8 %copy-start.4 = (s32[8,128]{1,0:T(8,128)S(1)}, s32[8,128]{1,0:T(8,128)}, u32[]{:S(2)}) copy-start(s32[8,128]{1,0:T(8,128)} %get-tuple-element.11.slots) | copy-start | bytes 12292
  3.1 43.4 %all-to-all-start = ((bf16[128,5,2,128]{3,2,1,0:T(2,128)(2,1)}), bf16[128,5,2,128]{3,2,1,0:T(2,128)(2,1)S(1)}, u32[]{:S(2)}, u32[]{:S(2)}) async-start(bf16[128,5,2,128]{3,2,1,0:T(2,128)(2,1)} %bitcast.28), calls=%async_computation | async-start | bytes 655360 | tf_op jit(solution)/shard_map/all_to_all | solution.py:449
  24.8 9.0 %collective-permute-start.2 = (bf16[64,1024]{1,0:T(8,128)(2,1)S(1)}, bf16[64,1024]{1,0:T(8,128)(2,1)S(1)}, u32[]{:S(2)}, u32[]{:S(2)}) collective-permute-start(bf16[64,1024]{1,0:T(8,128)(2,1)S(1)} %convert_bitcast_fusion.own), channel_id=1, source_target_pairs={{0,3},{1,2},{2,1},{3,0},{4,7},{5,6},{6,5},{7,4},{8,11},{9,10},{10,... | collective-permute-start | bytes 393224 | tf_op jit(solution)/shard_map/ppermute | solution.py:458
  29.2 7.5 %collective-permute-start.1 = (bf16[64,1024]{1,0:T(8,128)(2,1)S(1)}, bf16[64,1024]{1,0:T(8,128)(2,1)S(1)}, u32[]{:S(2)}, u32[]{:S(2)}) collective-permute-start(bf16[64,1024]{1,0:T(8,128)(2,1)S(1)} %convert_bitcast_fusion.own), channel_id=1, source_target_pairs={{0,2},{1,3},{2,0},{3,1},{4,6},{5,7},{6,4},{7,5},{8,10},{9,11},{10,... | collective-permute-start | bytes 393224 | tf_op jit(solution)/shard_map/ppermute | solution.py:458
  31.6 6.0 %collective-permute-start = (bf16[64,1024]{1,0:T(8,128)(2,1)S(1)}, bf16[64,1024]{1,0:T(8,128)(2,1)S(1)}, u32[]{:S(2)}, u32[]{:S(2)}) collective-permute-start(bf16[64,1024]{1,0:T(8,128)(2,1)S(1)} %convert_bitcast_fusion.own), channel_id=1, source_target_pairs={{0,1},{1,0},{2,3},{3,2},{4,5},{5,4},{6,7},{7,6},{8,9},{9,8},{10,11... | collective-permute-start | bytes 393224 | tf_op jit(solution)/shard_map/ppermute | solution.py:458
  37.6 1.0 copy-start.1
  38.6 0.9 copy-start.2
  39.6 0.9 copy-start.3
  97.9 22.0 %all-to-all-start.4 = ((bf16[128,2,2,128]{3,2,1,0:T(2,128)(2,1)}), bf16[128,2,2,128]{3,2,1,0:T(2,128)(2,1)S(1)}, u32[]{:S(2)}, u32[]{:S(2)}) async-start(bf16[128,2,2,128]{3,2,1,0:T(2,128)(2,1)} %bitcast.14), calls=%async_computation.4 | async-start | bytes 262144 | tf_op jit(solution)/shard_map/all_to_all | solution.py:449
